TPU v7x, 32 devices: a whole 2x2x4 slice. The times are simulated.
32 devices in a mesh: groups: 2 (over x), blk: 16 (over z, y, core).
Axes of the slice: x: 2, y: 2, z: 4, core: 2. Of those that a mesh axis runs over, the one named last changes fastest.
Arguments:
- points: bfloat16 [49152, 1024], P(('groups', 'blk')), parts along dimension 0, may hold values from -6 to 6
- coverage: float32 [49152], P(('groups', 'blk')), parts along dimension 0, may hold values from 0 to 1.5
- candidates: bfloat16 [4096, 1024], P(('groups', 'blk')), parts along dimension 0, may hold values from -6 to 6
- cand_count: int32 [32], P(('groups', 'blk')), parts along dimension 0, may hold values from 16 to 128, as said below
- acc_index: int32 [32, 16], P(('groups', 'blk')), parts along dimension 0, may hold values from 0 to 127, as said below
Outputs:
- gain_out: float32 [4096], P(('groups', 'blk')), parts along dimension 0
- new_coverage: float32 [49152], P(('groups', 'blk')), parts along dimension 0
There are 2 independent parts, one for each index of `groups`. A program takes and returns all parts, laid end to end along the dimension named above; each array names one. Nothing has to cross between parts.
Inputs may be any that keep to these rules, and one draw needn't show every extreme that they name: `cand_count`: some device has all 128 slots live. `acc_index`: each entry of row b is below cand_count[b]; entries may repeat.
All inputs are finite; a program needn't handle non-finite values.
Results may differ from a plain program's by a relative error of at most 0.0003.
Values may be sent and summed in bfloat16 or wider, within the bound.
No kernel may reach another device: no remote copies, remote signals or barrier semaphores. Data moves between devices by JAX's collectives and lax.ppermute only.
A program may use at most 64 MiB of HBM per device.

v0:
```python
import functools
import math

import jax
import jax.numpy as jnp
from jax import lax
from jax.experimental import pallas as pl
from jax.experimental.pallas import tpu as pltpu
from jax.sharding import PartitionSpec as P


F32 = jnp.float32
LANES = 128
SUBLANES = 8
CORES = 2
VMEM_SPEC = pl.BlockSpec(memory_space=pltpu.VMEM)


def chip_ring(mesh):
    row = mesh.devices.reshape(-1, mesh.shape["blk"])[0]
    natural = list(range(len(row) // CORES))
    coords = [getattr(row[CORES * c], "coords", None) for c in natural]
    if any(c is None for c in coords) or len({tuple(c)[:2] for c in coords}) == 1:
        return natural

    def near(a, b):
        return sum(abs(u - v) for u, v in zip(coords[a], coords[b])) == 1

    def grow(path, left):
        if not left:
            return path if near(path[-1], path[0]) else None
        for c in sorted(left):
            if near(path[-1], c):
                found = grow(path + [c], left - {c})
                if found:
                    return found
        return None

    return grow([0], frozenset(natural[1:])) or natural


def score_body(tile, halves, blocks, carried, *refs):
    refs = list(refs)

    def take(n):
        out, refs[:n] = refs[:n], []
        return out

    pts, covs, runs = take(halves), take(halves), take(halves)
    cands, biases, before = take(blocks), take(blocks), take(carried)
    new_runs, (out,) = take(halves), take(1)
    block = jnp.concatenate([c[...] for c in cands], axis=0)
    slots = cands[0].shape[0]
    rows = blocks * slots
    bias = jnp.concatenate(
        [jnp.broadcast_to(b[0:1, :], (slots, slots)).T[:, :LANES] for b in biases], axis=0
    )
    wide = jnp.concatenate([bias] * (tile // LANES), axis=1)
    total = before[0][...] if carried else jnp.zeros((rows, LANES), F32)
    for half in range(halves):
        for at in range(0, pts[half].shape[0], tile):
            span = pl.ds(at, tile)
            dots = lax.dot_general(
                block,
                pts[half][span, :],
                (((1,), (1,)), ((), ())),
                preferred_element_type=F32,
            )
            over = jnp.maximum(dots - covs[half][0:1, span], 0.0)
            for lane in range(0, tile, LANES):
                total = total + over[:, lane : lane + LANES]
            taken = (dots + wide).reshape(rows // SUBLANES, SUBLANES, tile)
            new_runs[half][:, span] = jnp.maximum(runs[half][:, span], jnp.max(taken, axis=0))
    if out.shape[0] == rows:
        out[...] = total
    else:
        for b in range(blocks):
            part = total[b * slots : (b + 1) * slots]
            out[b : b + 1, :] = jnp.sum(part.T, axis=0, keepdims=True)


def score(pts, covs, runs, cands, biases, before=None, last=True):
    halves, blocks = len(pts), len(cands)
    slots, width = cands[0].shape
    points = pts[0].shape[0]
    tile = math.gcd(points, 256)
    carried = () if before is None else (before,)
    out_rows = blocks if last else blocks * slots
    out = pl.pallas_call(
        functools.partial(score_body, tile, halves, blocks, len(carried)),
        out_shape=[jax.ShapeDtypeStruct(r.shape, F32) for r in runs]
        + [jax.ShapeDtypeStruct((out_rows, slots if last else LANES), F32)],
        in_specs=[VMEM_SPEC] * (3 * halves + 2 * blocks + len(carried)),
        out_specs=[VMEM_SPEC] * (halves + 1),
        input_output_aliases={2 * halves + h: h for h in range(halves)},
        compiler_params=pltpu.CompilerParams(vmem_limit_bytes=16 << 20),
        cost_estimate=pl.CostEstimate(
            flops=2 * blocks * slots * halves * points * width,
            bytes_accessed=halves * points * width * 2,
            transcendentals=0,
        ),
    )(*pts, *covs, *runs, *cands, *biases, *carried)
    return list(out[:halves]), out[halves]


def per_device(ring, points, coverage, candidates, cand_count, acc_index):
    width = points.shape[1]
    slots = candidates.shape[0]
    chips = len(ring)
    devices = chips * CORES
    root = math.sqrt(width)
    at = {c: p for p, c in enumerate(ring)}

    def move(x, step, cross):
        pairs = []
        for i in range(devices):
            chip, core = divmod(i, CORES)
            to = ring[(at[chip] + (step if core == 0 else -step)) % chips]
            pairs.append((i, to * CORES + (core ^ cross)))
        return lax.ppermute(x, "blk", pairs)

    def swap(x):
        return move(x, 0, 1)

    slot_ids = jnp.arange(slots, dtype=jnp.int32)
    marked = jnp.any(acc_index[0][:, None] == slot_ids[None, :], axis=0)
    bias = jnp.broadcast_to(jnp.where(marked, 0.0, -jnp.inf), (SUBLANES, slots)).astype(F32)
    cov = (coverage * root)[None, :]

    pts = [points, swap(points)]
    covs = [cov, swap(cov)]
    low = jnp.full((SUBLANES, points.shape[0]), -jnp.inf, F32)
    blocks, offsets = {}, {}
    for k in range(1, chips):
        hop = (k + 1) // 2
        step = (1 if k % 2 else -1) * (1 if hop % 2 else -1)
        source = (candidates, bias) if k <= 2 else blocks[k - 2]
        blocks[k] = (move(source[0], step, 1), move(source[1], step, 1))
        offsets[k] = (step * hop) % chips
    run_a, total = score(pts[:1], covs[:1], [low], [candidates], [bias], last=False)
    run_b, own = score(pts[1:], covs[1:], [low], [candidates], [bias], before=total)
    runs = run_a + run_b
    parts = {0: own}
    for k in range(2, chips + 1, 2):
        ks = [j for j in (k - 1, k) if j < chips]
        runs, sums = score(pts, covs, runs, [blocks[j][0] for j in ks], [blocks[j][1] for j in ks])
        for row, j in enumerate(ks):
            parts[offsets[j]] = sums[row : row + 1]
    h = 1
    while h < chips:
        cross = 1 if h == 1 else 0
        send = [e for e in sorted(parts) if e % (2 * h) == h]
        came = move(jnp.concatenate([parts.pop(e) for e in send], axis=0), h, cross)
        for row, e in enumerate(send):
            to = (1 - e if cross else e - h) % chips
            parts[to] = parts[to] + came[row : row + 1]
        h *= 2
    other = swap(jnp.max(runs[1], axis=0))
    best = jnp.maximum(jnp.max(runs[0], axis=0), other)
    new_coverage = jnp.maximum(coverage, best / root)
    live = slot_ids < cand_count[0]
    total = F32(points.shape[0] * devices) * root
    return jnp.where(live, parts[0][0] / total, 0.0), new_coverage


def solution(mesh):
    split = P(("groups", "blk"))
    wide = P(("groups", "blk"), None)
    ring = chip_ring(mesh)

    def body(*args):
        return per_device(ring, *args)

    return jax.shard_map(
        body,
        mesh=mesh,
        in_specs=(wide, split, wide, split, wide),
        out_specs=(split, split),
        check_vma=False,
    )
```

profile of v0, /device:TPU:0, one launch (start us, length us, event | category | flops | bytes accessed | tf_op | source)
XLA Modules:
  0.0 55.8 jit_solution(259877697762352470)
XLA Ops:
  0.6 0.6 collective-permute-start
  1.2 2.6 %collective-permute-start.2 = (bf16[128,1024]{1,0:T(8,128)(2,1)}, bf16[128,1024]{1,0:T(8,128)(2,1)S(1)}, u32[]{:S(2)}, u32[]{:S(2)}) collective-permute-start(bf16[128,1024]{1,0:T(8,128)(2,1)} %refs_3_.3), channel_id=1, source_target_pairs={{0,3},{1,4},{2,7},{3,0},{4,1},{5,8},{6,11},{7,2},{8,5},{9,12},{10,... | collective-permute-start | bytes 786440 | tf_op jit(solution)/shard_map/ppermute | solution.py:120
  3.8 1.3 %collective-permute-start.3 = (bf16[128,1024]{1,0:T(8,128)(2,1)}, bf16[128,1024]{1,0:T(8,128)(2,1)S(1)}, u32[]{:S(2)}, u32[]{:S(2)}) collective-permute-start(bf16[128,1024]{1,0:T(8,128)(2,1)} %refs_3_.3), channel_id=1, source_target_pairs={{0,5},{1,2},{2,1},{3,6},{4,9},{5,0},{6,3},{7,10},{8,13},{9,4},{10,... | collective-permute-start | bytes 786440 | tf_op jit(solution)/shard_map/ppermute | solution.py:120
  5.1 0.7 %fusion = pred[128]{0:T(512)(128)(4,1)S(1)} fusion(s32[16]{0:T(128)} %bitcast.5), kind=kLoop, calls=%fused_computation.2 | loop fusion | flops 3968 | bytes 192 | tf_op jit(solution)/shard_map/reduce_or | solution.py:126
  5.9 1.6 %collective-permute-start.4 = (f32[8,128]{1,0:T(8,128)S(1)}, f32[8,128]{1,0:T(8,128)S(1)}, u32[]{:S(2)}, u32[]{:S(2)}) collective-permute-start(f32[8,128]{1,0:T(8,128)S(1)} %broadcast_in_dim.24.refs_4_), channel_id=1, source_target_pairs={{0,3},{1,4},{2,7},{3,0},{4,1},{5,8},{6,11},{7,2},{8,5},{9,12},{10,... | collective-permute-start | bytes 12296 | tf_op jit(solution)/shard_map/ppermute | solution.py:120
  7.5 2.3 %collective-permute-done.2.refs_6_ = bf16[128,1024]{1,0:T(8,128)(2,1)S(1)} collective-permute-done((bf16[128,1024]{1,0:T(8,128)(2,1)}, bf16[128,1024]{1,0:T(8,128)(2,1)S(1)}, u32[]{:S(2)}, u32[]{:S(2)}) %collective-permute-start.2) | collective-permute-done | bytes 262176 | tf_op jit(solution)/shard_map/ppermute | solution.py:120
  9.8 2.6 %collective-permute-start.6 = (bf16[128,1024]{1,0:T(8,128)(2,1)S(1)}, bf16[128,1024]{1,0:T(8,128)(2,1)S(1)}, u32[]{:S(2)}, u32[]{:S(2)}) collective-permute-start(bf16[128,1024]{1,0:T(8,128)(2,1)S(1)} %collective-permute-done.2.refs_6_), channel_id=1, source_target_pairs={{0,5},{1,2},{2,1},{3,6},{4,9},{5,0},{6,3},{7,10},{8,13},{9,4},{10,... | collective-permute-start | bytes 786440 | tf_op jit(solution)/shard_map/ppermute | solution.py:120
  12.4 0.0 collective-permute-done.3.refs_7_
  12.4 0.3 collective-permute-start.7
  12.7 0.7 %broadcast_multiply_fusion = f32[1536]{0:T(1024)S(1)} fusion(f32[1536]{0:T(1024)} %param.6), kind=kLoop, calls=%fused_computation.3 | loop fusion | flops 1536 | bytes 12288 | tf_op jit(solution)/shard_map/mul | solution.py:128
  13.4 1.5 %collective-permute-start.1 = (f32[1,1536]{1,0:T(1,128)S(1)}, f32[1,1536]{1,0:T(1,128)S(1)}, u32[]{:S(2)}, u32[]{:S(2)}) collective-permute-start(f32[1,1536]{1,0:T(1,128)S(1)} %broadcast_in_dim.20.refs_1_.refs_2_), channel_id=1, source_target_pairs={{0,1},{1,0},{2,3},{3,2},{4,5},{5,4},{6,7},{7,6},{8,9},{9,8},{10,11... | collective-permute-start | bytes 18440 | tf_op jit(solution)/shard_map/ppermute | solution.py:120
  14.9 0.0 collective-permute-done.4.refs_8_
  14.9 1.5 %collective-permute-start.5 = (f32[8,128]{1,0:T(8,128)S(1)}, f32[8,128]{1,0:T(8,128)S(1)}, u32[]{:S(2)}, u32[]{:S(2)}) collective-permute-start(f32[8,128]{1,0:T(8,128)S(1)} %broadcast_in_dim.24.refs_4_), channel_id=1, source_target_pairs={{0,5},{1,2},{2,1},{3,6},{4,9},{5,0},{6,3},{7,10},{8,13},{9,4},{10,... | collective-permute-start | bytes 12296 | tf_op jit(solution)/shard_map/ppermute | solution.py:120
  16.4 1.8 %collective-permute-done.5.refs_9_ = f32[8,128]{1,0:T(8,128)S(1)} collective-permute-done((f32[8,128]{1,0:T(8,128)S(1)}, f32[8,128]{1,0:T(8,128)S(1)}, u32[]{:S(2)}, u32[]{:S(2)}) %collective-permute-start.5) | collective-permute-done | bytes 4128 | tf_op jit(solution)/shard_map/ppermute | solution.py:120
  18.1 2.2 %collective-permute-start.8 = (f32[8,128]{1,0:T(8,128)S(1)}, f32[8,128]{1,0:T(8,128)S(1)}, u32[]{:S(2)}, u32[]{:S(2)}) collective-permute-start(f32[8,128]{1,0:T(8,128)S(1)} %collective-permute-done.4.refs_8_), channel_id=1, source_target_pairs={{0,5},{1,2},{2,1},{3,6},{4,9},{5,0},{6,3},{7,10},{8,13},{9,4},{10,... | collective-permute-start | bytes 12296 | tf_op jit(solution)/shard_map/ppermute | solution.py:120
  20.3 0.0 collective-permute-done.1.refs_1_.refs_3_
  20.3 0.0 collective-permute-start.9
  20.4 0.0 copy-start
  20.4 1.9 %copy-done = bf16[1536,1024]{1,0:T(8,128)(2,1)S(1)} copy-done((bf16[1536,1024]{1,0:T(8,128)(2,1)S(1)}, bf16[1536,1024]{1,0:T(8,128)(2,1)}, u32[]{:S(2)}) %copy-start) | copy-done | bytes 3145752
  22.3 0.0 copy-start.2
  22.3 0.9 %copy-done.2 = bf16[128,1024]{1,0:T(8,128)(2,1)S(1)} copy-done((bf16[128,1024]{1,0:T(8,128)(2,1)S(1)}, bf16[128,1024]{1,0:T(8,128)(2,1)}, u32[]{:S(2)}) %copy-start.2) | copy-done | bytes 262168
  23.2 0.0 copy-start.1
  23.2 1.2 %shard_map.68 = (f32[8,1536]{1,0:T(8,128)S(1)}, f32[128,128]{1,0:T(8,128)S(1)}) custom-call(bf16[1536,1024]{1,0:T(8,128)(2,1)S(1)} %copy-done, f32[1,1536]{1,0:T(1,128)S(1)} %broadcast_in_dim.20.refs_1_.refs_2_, f32[8,1536]{1,0:T(8,128)S(1)} %broadcast_in_dim.21.clone.refs_2_, bf16[128,1024]{1,0:T(8,128)(2,1)S(1)} %copy-done.2, ...), custom_call_target="tpu_custom_call", output_to_operand_aliasing={{0}: (2, {})} | custom-call | flops 402653184 | bytes 3145728 | tf_op jit(solution)/shard_map/pallas_call | solution.py:89
  24.4 0.0 collective-permute-done.8.refs_8_
  24.4 1.8 %collective-permute-start.12 = (f32[8,128]{1,0:T(8,128)S(1)}, f32[8,128]{1,0:T(8,128)S(1)}, u32[]{:S(2)}, u32[]{:S(2)}) collective-permute-start(f32[8,128]{1,0:T(8,128)S(1)} %collective-permute-done.8.refs_8_), channel_id=1, source_target_pairs={{0,3},{1,4},{2,7},{3,0},{4,1},{5,8},{6,11},{7,2},{8,5},{9,12},{10,... | collective-permute-start | bytes 12296 | tf_op jit(solution)/shard_map/ppermute | solution.py:120
  26.2 0.0 collective-permute-done.9.refs_9_
  26.2 1.5 %collective-permute-start.13 = (f32[8,128]{1,0:T(8,128)S(1)}, f32[8,128]{1,0:T(8,128)S(1)}, u32[]{:S(2)}, u32[]{:S(2)}) collective-permute-start(f32[8,128]{1,0:T(8,128)S(1)} %collective-permute-done.9.refs_9_), channel_id=1, source_target_pairs={{0,5},{1,2},{2,1},{3,6},{4,9},{5,0},{6,3},{7,10},{8,13},{9,4},{10,... | collective-permute-start | bytes 12296 | tf_op jit(solution)/shard_map/ppermute | solution.py:120
  27.7 0.0 collective-permute-done.6.refs_6_
  27.7 0.0 collective-permute-start.10
  27.7 0.0 collective-permute-done.7.refs_7_
  27.7 1.7 %collective-permute-start.11 = (bf16[128,1024]{1,0:T(8,128)(2,1)S(1)}, bf16[128,1024]{1,0:T(8,128)(2,1)S(1)}, u32[]{:S(2)}, u32[]{:S(2)}) collective-permute-start(bf16[128,1024]{1,0:T(8,128)(2,1)S(1)} %collective-permute-done.7.refs_7_), channel_id=1, source_target_pairs={{0,5},{1,2},{2,1},{3,6},{4,9},{5,0},{6,3},{7,10},{8,13},{9,4},{10,... | collective-permute-start | bytes 786440 | tf_op jit(solution)/shard_map/ppermute | solution.py:120
  29.5 0.0 collective-permute-done.refs_0_.refs_1_
  29.5 1.3 %shard_map.69 = (f32[8,1536]{1,0:T(8,128)S(1)}, f32[1,128]{1,0:T(1,128)S(1)}) custom-call(bf16[1536,1024]{1,0:T(8,128)(2,1)S(1)} %collective-permute-done.refs_0_.refs_1_, f32[1,1536]{1,0:T(1,128)S(1)} %collective-permute-done.1.refs_1_.refs_3_, f32[8,1536]{1,0:T(8,128)S(1)} %broadcast_in_dim.21.refs_2_, ...), custom_call_target="tpu_custom_call", output_to_operand_aliasing={{0}: (2, {})} | custom-call | flops 402653184 | bytes 3145728 | tf_op jit(solution)/shard_map/pallas_call | solution.py:89
  30.7 0.0 copy-done.1
  30.8 2.1 %shard_map.70 = (f32[8,1536]{1,0:T(8,128)S(1)}, f32[8,1536]{1,0:T(8,128)S(1)}, f32[2,128]{1,0:T(2,128)S(1)}) custom-call(bf16[1536,1024]{1,0:T(8,128)(2,1)S(1)} %copy-done.1, bf16[1536,1024]{1,0:T(8,128)(2,1)S(1)} %collective-permute-done.refs_0_.refs_1_, ...), custom_call_target="tpu_custom_call", output_to_operand_aliasing={{0}: (4, {}), {1}: (5, {})} | custom-call | flops 1610612736 | bytes 6291456 | tf_op jit(solution)/shard_map/pallas_call | solution.py:89
  32.9 2.1 %shard_map.71 = (f32[8,1536]{1,0:T(8,128)S(1)}, f32[8,1536]{1,0:T(8,128)S(1)}, f32[2,128]{1,0:T(2,128)S(1)}) custom-call(bf16[1536,1024]{1,0:T(8,128)(2,1)S(1)} %copy-done.1, bf16[1536,1024]{1,0:T(8,128)(2,1)S(1)} %collective-permute-done.refs_0_.refs_1_, ...), custom_call_target="tpu_custom_call", output_to_operand_aliasing={{0}: (4, {}), {1}: (5, {})} | custom-call | flops 1610612736 | bytes 6291456 | tf_op jit(solution)/shard_map/pallas_call | solution.py:89
  35.1 0.0 collective-permute-done.12.refs_8_
  35.1 0.0 collective-permute-done.13.refs_9_
  35.1 0.0 collective-permute-done.10.refs_6_
  35.1 0.8 %collective-permute-done.11.refs_7_ = bf16[128,1024]{1,0:T(8,128)(2,1)S(1)} collective-permute-done((bf16[128,1024]{1,0:T(8,128)(2,1)S(1)}, bf16[128,1024]{1,0:T(8,128)(2,1)S(1)}, u32[]{:S(2)}, u32[]{:S(2)}) %collective-permute-start.11) | collective-permute-done | bytes 262176 | tf_op jit(solution)/shard_map/ppermute | solution.py:120
  35.9 2.1 %shard_map.72 = (f32[8,1536]{1,0:T(8,128)S(1)}, f32[8,1536]{1,0:T(8,128)S(1)}, f32[2,128]{1,0:T(2,128)S(1)}) custom-call(bf16[1536,1024]{1,0:T(8,128)(2,1)S(1)} %copy-done.1, bf16[1536,1024]{1,0:T(8,128)(2,1)S(1)} %collective-permute-done.refs_0_.refs_1_, ...), custom_call_target="tpu_custom_call", output_to_operand_aliasing={{0}: (4, {}), {1}: (5, {})} | custom-call | flops 1610612736 | bytes 6291456 | tf_op jit(solution)/shard_map/pallas_call | solution.py:89
  38.1 0.5 collective-permute-start.14
  38.6 1.6 %collective-permute-start.17 = (f32[8,128]{1,0:T(8,128)S(1)}, f32[8,128]{1,0:T(8,128)S(1)}, u32[]{:S(2)}, u32[]{:S(2)}) collective-permute-start(f32[8,128]{1,0:T(8,128)S(1)} %collective-permute-done.12.refs_8_), channel_id=1, source_target_pairs={{0,5},{1,2},{2,1},{3,6},{4,9},{5,0},{6,3},{7,10},{8,13},{9,4},{10,... | collective-permute-start | bytes 12296 | tf_op jit(solution)/shard_map/ppermute | solution.py:120
  40.2 0.2 collective-permute-start.16
  40.4 0.8 %collective-permute-done.14 = f32[4,128]{1,0:T(4,128)S(1)} collective-permute-done((f32[4,128]{1,0:T(4,128)S(1)}, f32[4,128]{1,0:T(4,128)S(1)}, u32[]{:S(2)}, u32[]{:S(2)}) %collective-permute-start.14) | collective-permute-done | bytes 2080 | tf_op jit(solution)/shard_map/ppermute | solution.py:120
  41.2 2.5 %collective-permute-start.15 = (f32[2,128]{1,0:T(2,128)S(1)}, f32[2,128]{1,0:T(2,128)S(1)}, u32[]{:S(2)}, u32[]{:S(2)}) collective-permute-start(f32[2,128]{1,0:T(2,128)S(1)} %pad_maximum_fusion.1), channel_id=1, source_target_pairs={{0,6},{1,9},{2,10},{3,5},{4,2},{5,13},{6,14},{7,1},{8,0},{9,15},{1... | collective-permute-start | bytes 3080 | tf_op jit(solution)/shard_map/ppermute | solution.py:120
  43.7 0.0 collective-permute-done.17.refs_7_
  43.7 2.3 %collective-permute-done.16.refs_6_ = bf16[128,1024]{1,0:T(8,128)(2,1)S(1)} collective-permute-done((bf16[128,1024]{1,0:T(8,128)(2,1)S(1)}, bf16[128,1024]{1,0:T(8,128)(2,1)S(1)}, u32[]{:S(2)}, u32[]{:S(2)}) %collective-permute-start.16) | collective-permute-done | bytes 262176 | tf_op jit(solution)/shard_map/ppermute | solution.py:120
  46.0 0.0 copy-start.3
  46.0 2.3 %shard_map.73 = (f32[8,1536]{1,0:T(8,128)S(1)}, f32[8,1536]{1,0:T(8,128)S(1)}, f32[1,128]{1,0:T(1,128)S(1)}) custom-call(bf16[1536,1024]{1,0:T(8,128)(2,1)S(1)} %copy-done.1, bf16[1536,1024]{1,0:T(8,128)(2,1)S(1)} %collective-permute-done.refs_0_.refs_1_, ...), custom_call_target="tpu_custom_call", output_to_operand_aliasing={{0}: (4, {}), {1}: (5, {})} | custom-call | flops 805306368 | bytes 6291456 | tf_op jit(solution)/shard_map/pallas_call | solution.py:89
  48.3 0.0 collective-permute-done.15
  48.3 3.2 %collective-permute-start.18 = (f32[1,128]{1,0:T(1,128)S(1)}, f32[1,128]{1,0:T(1,128)S(1)}, u32[]{:S(2)}, u32[]{:S(2)}) collective-permute-start(f32[1,128]{1,0:T(1,128)S(1)} %slice_add_fusion), channel_id=1, source_target_pairs={{0,14},{1,15},{2,12},{3,13},{4,10},{5,11},{6,8},{7,9},{8,6},{9,7},... | collective-permute-start | bytes 1544 | tf_op jit(solution)/shard_map/ppermute | solution.py:120
  52.2 0.1 collective-permute-start.19
  52.3 2.4 %collective-permute-done.18 = f32[1,128]{1,0:T(1,128)S(1)} collective-permute-done((f32[1,128]{1,0:T(1,128)S(1)}, f32[1,128]{1,0:T(1,128)S(1)}, u32[]{:S(2)}, u32[]{:S(2)}) %collective-permute-start.18) | collective-permute-done | bytes 544 | tf_op jit(solution)/shard_map/ppermute | solution.py:120
  54.7 0.5 compare_select_fusion
  55.2 0.0 collective-permute-done.19
  55.2 0.0 copy-done.3
  55.2 0.6 %multiply_maximum_fusion = f32[1536]{0:T(1024)} fusion(f32[1536]{0:T(1024)S(1)} %copy-done.3, f32[1536]{0:T(1024)S(1)} %reduce_max.18, f32[1536]{0:T(1024)S(1)} %collective-permute-done.19), kind=kLoop, calls=%fused_computation | loop fusion | flops 4608 | bytes 24576 | tf_op jit(solution)/shard_map/max | solution.py:160
  (12 shorter events, 0.1 us)
Async XLA Ops:
  0.6 28.8 %collective-permute-start = (bf16[1536,1024]{1,0:T(8,128)(2,1)}, bf16[1536,1024]{1,0:T(8,128)(2,1)S(1)}, u32[]{:S(2)}, u32[]{:S(2)}) collective-permute-start(bf16[1536,1024]{1,0:T(8,128)(2,1)} %refs_0_.9), channel_id=1, source_target_pairs={{0,1},{1,0},{2,3},{3,2},{4,5},{5,4},{6,7},{7,6},{8,9},{9,8},{10,11... | collective-permute-start | bytes 9437192 | tf_op jit(solution)/shard_map/ppermute | solution.py:120
  1.2 8.6 %collective-permute-start.2 = (bf16[128,1024]{1,0:T(8,128)(2,1)}, bf16[128,1024]{1,0:T(8,128)(2,1)S(1)}, u32[]{:S(2)}, u32[]{:S(2)}) collective-permute-start(bf16[128,1024]{1,0:T(8,128)(2,1)} %refs_3_.3), channel_id=1, source_target_pairs={{0,3},{1,4},{2,7},{3,0},{4,1},{5,8},{6,11},{7,2},{8,5},{9,12},{10,... | collective-permute-start | bytes 786440 | tf_op jit(solution)/shard_map/ppermute | solution.py:120
  3.8 8.6 %collective-permute-start.3 = (bf16[128,1024]{1,0:T(8,128)(2,1)}, bf16[128,1024]{1,0:T(8,128)(2,1)S(1)}, u32[]{:S(2)}, u32[]{:S(2)}) collective-permute-start(bf16[128,1024]{1,0:T(8,128)(2,1)} %refs_3_.3), channel_id=1, source_target_pairs={{0,5},{1,2},{2,1},{3,6},{4,9},{5,0},{6,3},{7,10},{8,13},{9,4},{10,... | collective-permute-start | bytes 786440 | tf_op jit(solution)/shard_map/ppermute | solution.py:120
  5.9 9.0 %collective-permute-start.4 = (f32[8,128]{1,0:T(8,128)S(1)}, f32[8,128]{1,0:T(8,128)S(1)}, u32[]{:S(2)}, u32[]{:S(2)}) collective-permute-start(f32[8,128]{1,0:T(8,128)S(1)} %broadcast_in_dim.24.refs_4_), channel_id=1, source_target_pairs={{0,3},{1,4},{2,7},{3,0},{4,1},{5,8},{6,11},{7,2},{8,5},{9,12},{10,... | collective-permute-start | bytes 12296 | tf_op jit(solution)/shard_map/ppermute | solution.py:120
  9.8 17.9 %collective-permute-start.6 = (bf16[128,1024]{1,0:T(8,128)(2,1)S(1)}, bf16[128,1024]{1,0:T(8,128)(2,1)S(1)}, u32[]{:S(2)}, u32[]{:S(2)}) collective-permute-start(bf16[128,1024]{1,0:T(8,128)(2,1)S(1)} %collective-permute-done.2.refs_6_), channel_id=1, source_target_pairs={{0,5},{1,2},{2,1},{3,6},{4,9},{5,0},{6,3},{7,10},{8,13},{9,4},{10,... | collective-permute-start | bytes 786440 | tf_op jit(solution)/shard_map/ppermute | solution.py:120
  12.4 15.3 %collective-permute-start.7 = (bf16[128,1024]{1,0:T(8,128)(2,1)S(1)}, bf16[128,1024]{1,0:T(8,128)(2,1)S(1)}, u32[]{:S(2)}, u32[]{:S(2)}) collective-permute-start(bf16[128,1024]{1,0:T(8,128)(2,1)S(1)} %collective-permute-done.3.refs_7_), channel_id=1, source_target_pairs={{0,3},{1,4},{2,7},{3,0},{4,1},{5,8},{6,11},{7,2},{8,5},{9,12},{10,... | collective-permute-start | bytes 786440 | tf_op jit(solution)/shard_map/ppermute | solution.py:120
  13.4 6.9 %collective-permute-start.1 = (f32[1,1536]{1,0:T(1,128)S(1)}, f32[1,1536]{1,0:T(1,128)S(1)}, u32[]{:S(2)}, u32[]{:S(2)}) collective-permute-start(f32[1,1536]{1,0:T(1,128)S(1)} %broadcast_in_dim.20.refs_1_.refs_2_), channel_id=1, source_target_pairs={{0,1},{1,0},{2,3},{3,2},{4,5},{5,4},{6,7},{7,6},{8,9},{9,8},{10,11... | collective-permute-start | bytes 18440 | tf_op jit(solution)/shard_map/ppermute | solution.py:120
  14.9 3.3 %collective-permute-start.5 = (f32[8,128]{1,0:T(8,128)S(1)}, f32[8,128]{1,0:T(8,128)S(1)}, u32[]{:S(2)}, u32[]{:S(2)}) collective-permute-start(f32[8,128]{1,0:T(8,128)S(1)} %broadcast_in_dim.24.refs_4_), channel_id=1, source_target_pairs={{0,5},{1,2},{2,1},{3,6},{4,9},{5,0},{6,3},{7,10},{8,13},{9,4},{10,... | collective-permute-start | bytes 12296 | tf_op jit(solution)/shard_map/ppermute | solution.py:120
  18.1 6.3 %collective-permute-start.8 = (f32[8,128]{1,0:T(8,128)S(1)}, f32[8,128]{1,0:T(8,128)S(1)}, u32[]{:S(2)}, u32[]{:S(2)}) collective-permute-start(f32[8,128]{1,0:T(8,128)S(1)} %collective-permute-done.4.refs_8_), channel_id=1, source_target_pairs={{0,5},{1,2},{2,1},{3,6},{4,9},{5,0},{6,3},{7,10},{8,13},{9,4},{10,... | collective-permute-start | bytes 12296 | tf_op jit(solution)/shard_map/ppermute | solution.py:120
  20.3 5.9 %collective-permute-start.9 = (f32[8,128]{1,0:T(8,128)S(1)}, f32[8,128]{1,0:T(8,128)S(1)}, u32[]{:S(2)}, u32[]{:S(2)}) collective-permute-start(f32[8,128]{1,0:T(8,128)S(1)} %collective-permute-done.5.refs_9_), channel_id=1, source_target_pairs={{0,3},{1,4},{2,7},{3,0},{4,1},{5,8},{6,11},{7,2},{8,5},{9,12},{10,... | collective-permute-start | bytes 12296 | tf_op jit(solution)/shard_map/ppermute | solution.py:120
  20.4 1.9 %copy-start = (bf16[1536,1024]{1,0:T(8,128)(2,1)S(1)}, bf16[1536,1024]{1,0:T(8,128)(2,1)}, u32[]{:S(2)}) copy-start(bf16[1536,1024]{1,0:T(8,128)(2,1)} %refs_0_.9) | copy-start | bytes 9437188
  22.3 0.9 %copy-start.2 = (bf16[128,1024]{1,0:T(8,128)(2,1)S(1)}, bf16[128,1024]{1,0:T(8,128)(2,1)}, u32[]{:S(2)}) copy-start(bf16[128,1024]{1,0:T(8,128)(2,1)} %refs_3_.3) | copy-start | bytes 786436
  23.2 7.5 %copy-start.1 = (bf16[1536,1024]{1,0:T(8,128)(2,1)S(1)}, bf16[1536,1024]{1,0:T(8,128)(2,1)}, u32[]{:S(2)}) copy-start(bf16[1536,1024]{1,0:T(8,128)(2,1)} %refs_0_.9) | copy-start | bytes 9437188
  24.4 10.7 %collective-permute-start.12 = (f32[8,128]{1,0:T(8,128)S(1)}, f32[8,128]{1,0:T(8,128)S(1)}, u32[]{:S(2)}, u32[]{:S(2)}) collective-permute-start(f32[8,128]{1,0:T(8,128)S(1)} %collective-permute-done.8.refs_8_), channel_id=1, source_target_pairs={{0,3},{1,4},{2,7},{3,0},{4,1},{5,8},{6,11},{7,2},{8,5},{9,12},{10,... | collective-permute-start | bytes 12296 | tf_op jit(solution)/shard_map/ppermute | solution.py:120
  26.2 8.9 %collective-permute-start.13 = (f32[8,128]{1,0:T(8,128)S(1)}, f32[8,128]{1,0:T(8,128)S(1)}, u32[]{:S(2)}, u32[]{:S(2)}) collective-permute-start(f32[8,128]{1,0:T(8,128)S(1)} %collective-permute-done.9.refs_9_), channel_id=1, source_target_pairs={{0,5},{1,2},{2,1},{3,6},{4,9},{5,0},{6,3},{7,10},{8,13},{9,4},{10,... | collective-permute-start | bytes 12296 | tf_op jit(solution)/shard_map/ppermute | solution.py:120
  27.7 7.4 %collective-permute-start.10 = (bf16[128,1024]{1,0:T(8,128)(2,1)S(1)}, bf16[128,1024]{1,0:T(8,128)(2,1)S(1)}, u32[]{:S(2)}, u32[]{:S(2)}) collective-permute-start(bf16[128,1024]{1,0:T(8,128)(2,1)S(1)} %collective-permute-done.6.refs_6_), channel_id=1, source_target_pairs={{0,3},{1,4},{2,7},{3,0},{4,1},{5,8},{6,11},{7,2},{8,5},{9,12},{10,... | collective-permute-start | bytes 786440 | tf_op jit(solution)/shard_map/ppermute | solution.py:120
  27.7 8.2 %collective-permute-start.11 = (bf16[128,1024]{1,0:T(8,128)(2,1)S(1)}, bf16[128,1024]{1,0:T(8,128)(2,1)S(1)}, u32[]{:S(2)}, u32[]{:S(2)}) collective-permute-start(bf16[128,1024]{1,0:T(8,128)(2,1)S(1)} %collective-permute-done.7.refs_7_), channel_id=1, source_target_pairs={{0,5},{1,2},{2,1},{3,6},{4,9},{5,0},{6,3},{7,10},{8,13},{9,4},{10,... | collective-permute-start | bytes 786440 | tf_op jit(solution)/shard_map/ppermute | solution.py:120
  38.1 3.1 %collective-permute-start.14 = (f32[4,128]{1,0:T(4,128)S(1)}, f32[4,128]{1,0:T(4,128)S(1)}, u32[]{:S(2)}, u32[]{:S(2)}) collective-permute-start(f32[4,128]{1,0:T(4,128)S(1)} %pad_maximum_fusion), channel_id=1, source_target_pairs={{0,3},{1,4},{2,7},{3,0},{4,1},{5,8},{6,11},{7,2},{8,5},{9,12},{10,... | collective-permute-start | bytes 6152 | tf_op jit(solution)/shard_map/ppermute | solution.py:120
  38.6 5.1 %collective-permute-start.17 = (f32[8,128]{1,0:T(8,128)S(1)}, f32[8,128]{1,0:T(8,128)S(1)}, u32[]{:S(2)}, u32[]{:S(2)}) collective-permute-start(f32[8,128]{1,0:T(8,128)S(1)} %collective-permute-done.12.refs_8_), channel_id=1, source_target_pairs={{0,5},{1,2},{2,1},{3,6},{4,9},{5,0},{6,3},{7,10},{8,13},{9,4},{10,... | collective-permute-start | bytes 12296 | tf_op jit(solution)/shard_map/ppermute | solution.py:120
  40.2 5.8 %collective-permute-start.16 = (bf16[128,1024]{1,0:T(8,128)(2,1)S(1)}, bf16[128,1024]{1,0:T(8,128)(2,1)S(1)}, u32[]{:S(2)}, u32[]{:S(2)}) collective-permute-start(bf16[128,1024]{1,0:T(8,128)(2,1)S(1)} %collective-permute-done.10.refs_6_), channel_id=1, source_target_pairs={{0,5},{1,2},{2,1},{3,6},{4,9},{5,0},{6,3},{7,10},{8,13},{9,4},{10,... | collective-permute-start | bytes 786440 | tf_op jit(solution)/shard_map/ppermute | solution.py:120
  41.2 7.1 %collective-permute-start.15 = (f32[2,128]{1,0:T(2,128)S(1)}, f32[2,128]{1,0:T(2,128)S(1)}, u32[]{:S(2)}, u32[]{:S(2)}) collective-permute-start(f32[2,128]{1,0:T(2,128)S(1)} %pad_maximum_fusion.1), channel_id=1, source_target_pairs={{0,6},{1,9},{2,10},{3,5},{4,2},{5,13},{6,14},{7,1},{8,0},{9,15},{1... | collective-permute-start | bytes 3080 | tf_op jit(solution)/shard_map/ppermute | solution.py:120
  46.0 9.2 %copy-start.3 = (f32[1536]{0:T(1024)S(1)}, f32[1536]{0:T(1024)}, u32[]{:S(2)}) copy-start(f32[1536]{0:T(1024)} %param.6) | copy-start | bytes 18436
  48.3 6.3 %collective-permute-start.18 = (f32[1,128]{1,0:T(1,128)S(1)}, f32[1,128]{1,0:T(1,128)S(1)}, u32[]{:S(2)}, u32[]{:S(2)}) collective-permute-start(f32[1,128]{1,0:T(1,128)S(1)} %slice_add_fusion), channel_id=1, source_target_pairs={{0,14},{1,15},{2,12},{3,13},{4,10},{5,11},{6,8},{7,9},{8,6},{9,7},... | collective-permute-start | bytes 1544 | tf_op jit(solution)/shard_map/ppermute | solution.py:120
  52.2 3.0 %collective-permute-start.19 = (f32[1536]{0:T(1024)S(1)}, f32[1536]{0:T(1024)S(1)}, u32[]{:S(2)}, u32[]{:S(2)}) collective-permute-start(f32[1536]{0:T(1024)S(1)} %reduce_max.19), channel_id=1, source_target_pairs={{0,1},{1,0},{2,3},{3,2},{4,5},{5,4},{6,7},{7,6},{8,9},{9,8},{10,11... | collective-permute-start | bytes 18440 | tf_op jit(solution)/shard_map/ppermute | solution.py:120
where the time goes:
time: 56 us; the launch traced here: 55.8 us
  starting transfers between devices  27.3 us (49%)
  Pallas kernels  11.2 us (20%)
  waiting for transfers between devices  10.4 us (19%)
  local copies, waits for them, and re-layouts  2.87 us (5%)
  other arithmetic  2.64 us (5%)
  between operations  1.42 us (3%)
    ppermute x20, starting transfers between devices, move(): return lax.ppermute(x, 'blk', pairs)  27.3 us
    pallas_call x6, Pallas kernels, score(): pl.pallas_call(functools.partial(score_body, tile, halves, blocks, len(ca...  11.2 us
    ppermute x20, waiting for transfers between devices, move(): return lax.ppermute(x, 'blk', pairs)  10.4 us
    unnamed x8, local copies, waits for them, and re-layouts  2.84 us
  transfers between devices with their start and end apart: 20, of which 6 were waited for; matrix products, arithmetic and copies ran while one was open for 4% of the time, Pallas kernels for 16%

commit v1 on v0

v1 whole, which is shorter than its diff:
```python
import functools
import math

import jax
import jax.numpy as jnp
from jax import lax
from jax.experimental import pallas as pl
from jax.experimental.pallas import tpu as pltpu
from jax.sharding import PartitionSpec as P


F32 = jnp.float32
LANES = 128
SUBLANES = 8
CORES = 2
VMEM_SPEC = pl.BlockSpec(memory_space=pltpu.VMEM)


def chip_ring(mesh):
    row = mesh.devices.reshape(-1, mesh.shape["blk"])[0]
    natural = list(range(len(row) // CORES))
    coords = [getattr(row[CORES * c], "coords", None) for c in natural]
    if any(c is None for c in coords) or len({tuple(c)[:2] for c in coords}) == 1:
        return natural

    def near(a, b):
        return sum(abs(u - v) for u, v in zip(coords[a], coords[b])) == 1

    def grow(path, left):
        if not left:
            return path if near(path[-1], path[0]) else None
        for c in sorted(left):
            if near(path[-1], c):
                found = grow(path + [c], left - {c})
                if found:
                    return found
        return None

    return grow([0], frozenset(natural[1:])) or natural


def bias_column(picks, slots):
    slot = lax.broadcasted_iota(jnp.int32, (slots, picks.shape[1]), 0)
    hit = jnp.where(slot == picks, 0.0, -jnp.inf)
    return jnp.max(hit, axis=1, keepdims=True)


def scan_points(block, bias, tiles, total):
    rows = block.shape[0]
    for load, cov, keep, store in tiles:
        dots = lax.dot_general(
            block, load(), (((1,), (1,)), ((), ())), preferred_element_type=F32
        )
        tile = dots.shape[1]
        over = jnp.maximum(dots - cov(), 0.0)
        for lane in range(0, tile, LANES):
            total = total + over[:, lane : lane + LANES]
        best = jnp.max((dots + bias).reshape(rows // SUBLANES, SUBLANES, tile), axis=0)
        store(best if keep is None else jnp.maximum(keep(), best))
    return total


def finish(total, slots, out):
    if out.shape[0] == total.shape[0]:
        out[...] = total
    else:
        for b in range(total.shape[0] // slots):
            part = total[b * slots : (b + 1) * slots]
            out[b : b + 1, :] = jnp.sum(part.T, axis=0, keepdims=True)


def tile_of(points):
    return math.gcd(points, 256)


def scale_body(root, cov, out):
    out[...] = cov[...] * root


def scaled(root, coverage, slack):
    return pl.pallas_call(
        functools.partial(scale_body, root),
        out_shape=jax.ShapeDtypeStruct((1, coverage.shape[0]), F32),
        in_specs=[VMEM_SPEC],
        out_specs=VMEM_SPEC,
        compiler_params=pltpu.CompilerParams(vmem_limit_bytes=4 << 20),
        cost_estimate=pl.CostEstimate(flops=slack, bytes_accessed=0, transcendentals=0),
    )(coverage[None, :])


def score_body(halves, blocks, fresh, carried, *refs):
    refs = list(refs)

    def take(n):
        got, refs[:n] = refs[:n], []
        return got

    pts, covs, runs = take(halves), take(halves), take(0 if fresh else halves)
    cands, picks, before = take(blocks), take(blocks), take(carried)
    new_runs, (out,) = take(halves), take(1)
    block = jnp.concatenate([c[...] for c in cands], axis=0)
    slots = cands[0].shape[0]
    bias = jnp.concatenate([bias_column(p[...], slots) for p in picks], axis=0)
    total = before[0][...] if carried else jnp.zeros((blocks * slots, LANES), F32)

    def keep(half, span):
        return runs[half][:, span]

    def store(half, span, x):
        new_runs[half][:, span] = x

    tiles = []
    for half in range(halves):
        tile = tile_of(pts[half].shape[0])
        for at in range(0, pts[half].shape[0], tile):
            span = pl.ds(at, tile)
            tiles.append(
                (
                    lambda half=half, span=span: pts[half][span, :],
                    lambda half=half, span=span: covs[half][0:1, span],
                    None if fresh else functools.partial(keep, half, span),
                    functools.partial(store, half, span),
                )
            )
    finish(scan_points(block, bias, tiles, total), slots, out)


def score(pts, covs, runs, cands, picks, before=None, last=True):
    halves, blocks = len(pts), len(cands)
    slots, width = cands[0].shape
    points = pts[0].shape[0]
    fresh = runs is None
    carried = () if before is None else (before,)
    run_shape = jax.ShapeDtypeStruct((SUBLANES, points), F32)
    out_shape = (blocks, slots) if last else (blocks * slots, LANES)
    kept = [] if fresh else runs
    out = pl.pallas_call(
        functools.partial(score_body, halves, blocks, fresh, len(carried)),
        out_shape=[run_shape] * halves + [jax.ShapeDtypeStruct(out_shape, F32)],
        in_specs=[VMEM_SPEC] * (2 * halves + len(kept) + 2 * blocks + len(carried)),
        out_specs=[VMEM_SPEC] * (halves + 1),
        input_output_aliases={} if fresh else {2 * halves + h: h for h in range(halves)},
        compiler_params=pltpu.CompilerParams(vmem_limit_bytes=16 << 20),
        cost_estimate=pl.CostEstimate(
            flops=2 * blocks * slots * halves * points * width,
            bytes_accessed=halves * points * width * 2,
            transcendentals=0,
        ),
    )(*pts, *covs, *kept, *cands, *picks, *carried)
    return list(out[:halves]), out[halves]


def per_device(ring, points, coverage, candidates, cand_count, acc_index):
    width = points.shape[1]
    slots = candidates.shape[0]
    chips = len(ring)
    devices = chips * CORES
    root = math.sqrt(width)
    at = {c: p for p, c in enumerate(ring)}

    def move(x, step, cross):
        pairs = []
        for i in range(devices):
            chip, core = divmod(i, CORES)
            to = ring[(at[chip] + (step if core == 0 else -step)) % chips]
            pairs.append((i, to * CORES + (core ^ cross)))
        return lax.ppermute(x, "blk", pairs)

    def swap(x):
        return move(x, 0, 1)

    cov = scaled(root, coverage, 32 * slots * points.shape[0] * width)
    pts = [points, swap(points)]
    covs = [cov, swap(cov)]
    alone = [candidates], [acc_index]
    run_a, total = score(pts[:1], covs[:1], None, *alone, last=False)
    run_b, gain = score(pts[1:], covs[1:], None, *alone, before=total)
    runs = run_a + run_b

    blocks, picks, parts, home = {}, {}, {}, {}
    for k in range(1, chips):
        hop = (k + 1) // 2
        step = (1 if k % 2 else -1) * (1 if hop % 2 else -1)
        home[k] = (step * hop) % chips
        blocks[k] = move(candidates if k <= 2 else blocks[k - 2], step, 1)
        picks[k] = move(acc_index if k <= 2 else picks[k - 2], step, 1)
    for k in range(2, chips + 1, 2):
        ks = [j for j in (k - 1, k) if j < chips]
        group = [blocks[j] for j in ks], [picks[j] for j in ks]
        if k < chips - 2:
            run_a, total = score(pts[:1], covs[:1], runs[:1], *group, last=False)
            run_b, sums = score(pts[1:], covs[1:], runs[1:], *group, before=total)
            runs = run_a + run_b
        else:
            runs, sums = score(pts, covs, runs, *group)
        parts.update({home[j]: sums[row : row + 1] for row, j in enumerate(ks)})
    odd = [e for e in sorted(parts) if e % 2]
    came = move(jnp.concatenate([parts[e] for e in odd], axis=0), 1, 1)
    for row, e in enumerate(odd):
        to = (1 - e) % chips
        if to:
            parts[to] = parts[to] + came[row : row + 1]
        else:
            gain = gain + came[row : row + 1]
    for e in sorted(parts):
        if e and e % 2 == 0:
            gain = gain + move(parts[e], e, 0)
    other = swap(jnp.max(runs[1], axis=0))
    best = jnp.maximum(jnp.max(runs[0], axis=0), other)
    new_coverage = jnp.maximum(coverage, best / root)
    live = jnp.arange(slots, dtype=jnp.int32) < cand_count[0]
    scale = F32(points.shape[0] * devices) * root
    return jnp.where(live, gain[0] / scale, 0.0), new_coverage


def solution(mesh):
    split = P(("groups", "blk"))
    wide = P(("groups", "blk"), None)
    ring = chip_ring(mesh)

    def body(*args):
        return per_device(ring, *args)

    return jax.shard_map(
        body,
        mesh=mesh,
        in_specs=(wide, split, wide, split, wide),
        out_specs=(split, split),
        check_vma=False,
    )
```

time: 56 us -> 51.8 us (0.925)
  waiting for transfers between devices: 10.4 us -> 7.81 us
  local copies, waits for them, and re-layouts: 2.87 us -> 0.77 us
  starting transfers between devices: 27.3 us -> 28.8 us
  other arithmetic: 2.64 us -> 1.18 us
    unnamed x8, local copies, waits for them, and re-layouts: 2.84 us -> 0.06 us
    ppermute x20 -> x21, waiting for transfers between devices: 10.4 us -> 7.81 us  [move(): return lax.ppermute(x, 'blk', pairs)]
    ppermute x20 -> x21, starting transfers between devices: 27.3 us -> 28.8 us  [move(): return lax.ppermute(x, 'blk', pairs)]
    reduce_or x1 -> x0, other arithmetic: 0.74 us -> none  [per_device(): marked = jnp.any(acc_index[0][:, None] == slot_ids[None, :], axis=0)]
    mul x1 -> x0, other arithmetic: 0.7 us -> none  [per_device(): cov = (coverage * root)[None, :]]
    broadcast_in_dim x4 -> x1, local copies, waits for them, and re-layouts: 0.02 us -> 0.7 us  [scaled(): coverage[None, :]]
    pallas_call x6 -> x9, Pallas kernels: 11.2 us -> 11.6 us  [the longest x8 11.6 us: score(): pl.pallas_call(functools.partial(score_body, halves, blocks, fresh, len(c...]
  transfers between devices with their start and end apart: 20 -> 21, of which waited for: 6 -> 5; matrix products, arithmetic and copies ran while one was open for 4% -> 2% of each run, Pallas kernels for 16% -> 23%
where the time goes in v1:
time: 51.8 us; the launch traced here: 51.6 us
  starting transfers between devices  28.8 us (56%)
  Pallas kernels  11.6 us (22%)
  waiting for transfers between devices  7.81 us (15%)
  between operations  1.42 us (3%)
  other arithmetic  1.18 us (2%)
  local copies, waits for them, and re-layouts  0.77 us (1%)
    ppermute x21, starting transfers between devices, move(): return lax.ppermute(x, 'blk', pairs)  28.8 us
    pallas_call x8, Pallas kernels, score(): pl.pallas_call(functools.partial(score_body, halves, blocks, fresh, len(c...  11.6 us
    ppermute x21, waiting for transfers between devices, move(): return lax.ppermute(x, 'blk', pairs)  7.81 us
  transfers between devices with their start and end apart: 21, of which 5 were waited for; matrix products, arithmetic and copies ran while one was open for 2% of the time, Pallas kernels for 23%

profile of v1, /device:TPU:0, one launch (start us, length us, event | category | flops | bytes accessed | tf_op | source)
XLA Modules:
  0.0 51.6 jit_solution(7144285321046803245)
XLA Ops:
  0.6 0.6 %collective-permute-start = (bf16[1536,1024]{1,0:T(8,128)(2,1)}, bf16[1536,1024]{1,0:T(8,128)(2,1)S(1)}, u32[]{:S(2)}, u32[]{:S(2)}) collective-permute-start(bf16[1536,1024]{1,0:T(8,128)(2,1)} %refs_0_.9), channel_id=1, source_target_pairs={{0,1},{1,0},{2,3},{3,2},{4,5},{5,4},{6,7},{7,6},{8,9},{9,8},{10,11... | collective-permute-start | bytes 9437192 | tf_op jit(solution)/shard_map/ppermute | solution.py:167
  1.2 2.6 %collective-permute-start.2 = (bf16[128,1024]{1,0:T(8,128)(2,1)}, bf16[128,1024]{1,0:T(8,128)(2,1)S(1)}, u32[]{:S(2)}, u32[]{:S(2)}) collective-permute-start(bf16[128,1024]{1,0:T(8,128)(2,1)} %refs_2_.3), channel_id=1, source_target_pairs={{0,3},{1,4},{2,7},{3,0},{4,1},{5,8},{6,11},{7,2},{8,5},{9,12},{10,... | collective-permute-start | bytes 786440 | tf_op jit(solution)/shard_map/ppermute | solution.py:167
  3.8 1.3 %collective-permute-start.3 = (bf16[128,1024]{1,0:T(8,128)(2,1)}, bf16[128,1024]{1,0:T(8,128)(2,1)S(1)}, u32[]{:S(2)}, u32[]{:S(2)}) collective-permute-start(bf16[128,1024]{1,0:T(8,128)(2,1)} %refs_2_.3), channel_id=1, source_target_pairs={{0,5},{1,2},{2,1},{3,6},{4,9},{5,0},{6,3},{7,10},{8,13},{9,4},{10,... | collective-permute-start | bytes 786440 | tf_op jit(solution)/shard_map/ppermute | solution.py:167
  5.1 4.7 %collective-permute-done.2.refs_3_ = bf16[128,1024]{1,0:T(8,128)(2,1)S(1)} collective-permute-done((bf16[128,1024]{1,0:T(8,128)(2,1)}, bf16[128,1024]{1,0:T(8,128)(2,1)S(1)}, u32[]{:S(2)}, u32[]{:S(2)}) %collective-permute-start.2) | collective-permute-done | bytes 262176 | tf_op jit(solution)/shard_map/ppermute | solution.py:167
  9.8 2.6 %collective-permute-start.6 = (bf16[128,1024]{1,0:T(8,128)(2,1)S(1)}, bf16[128,1024]{1,0:T(8,128)(2,1)S(1)}, u32[]{:S(2)}, u32[]{:S(2)}) collective-permute-start(bf16[128,1024]{1,0:T(8,128)(2,1)S(1)} %collective-permute-done.2.refs_3_), channel_id=1, source_target_pairs={{0,5},{1,2},{2,1},{3,6},{4,9},{5,0},{6,3},{7,10},{8,13},{9,4},{10,... | collective-permute-start | bytes 786440 | tf_op jit(solution)/shard_map/ppermute | solution.py:167
  12.4 0.3 collective-permute-start.4
  12.7 2.9 %collective-permute-start.5 = (s32[1,16]{1,0:T(1,128)}, s32[1,16]{1,0:T(1,128)S(1)}, u32[]{:S(2)}, u32[]{:S(2)}) collective-permute-start(s32[1,16]{1,0:T(1,128)} %refs_3_.3), channel_id=1, source_target_pairs={{0,5},{1,2},{2,1},{3,6},{4,9},{5,0},{6,3},{7,10},{8,13},{9,4},{10,... | collective-permute-start | bytes 200 | tf_op jit(solution)/shard_map/ppermute | solution.py:167
  15.6 0.7 %broadcast_in_dim.7.cov = f32[1,1536]{1,0:T(1,128)S(1)} reshape(f32[1536]{0:T(1024)} %param.6) | data formatting | bytes 12288 | tf_op jit(solution)/shard_map/broadcast_in_dim | solution.py:88
  16.3 0.0 copy-start
  16.3 0.0 copy-start.1
  16.3 0.0 copy-start.2
  16.3 0.0 collective-permute-done.3.refs_4_
  16.3 0.5 collective-permute-start.7
  16.8 0.0 collective-permute-done.6.refs_3_
  16.8 1.3 %collective-permute-start.10 = (bf16[128,1024]{1,0:T(8,128)(2,1)S(1)}, bf16[128,1024]{1,0:T(8,128)(2,1)S(1)}, u32[]{:S(2)}, u32[]{:S(2)}) collective-permute-start(bf16[128,1024]{1,0:T(8,128)(2,1)S(1)} %collective-permute-done.6.refs_3_), channel_id=1, source_target_pairs={{0,3},{1,4},{2,7},{3,0},{4,1},{5,8},{6,11},{7,2},{8,5},{9,12},{10,... | collective-permute-start | bytes 786440 | tf_op jit(solution)/shard_map/ppermute | solution.py:167
  18.1 0.0 copy-done
  18.2 0.0 copy-done.1
  18.2 0.0 copy-done.2
  18.2 1.2 %shard_map.69 = (f32[8,1536]{1,0:T(8,128)S(1)}, f32[128,128]{1,0:T(8,128)S(1)}) custom-call(bf16[1536,1024]{1,0:T(8,128)(2,1)S(1)} %copy-done, f32[1,1536]{1,0:T(1,128)S(1)} %shard_map.68.refs_1_.refs_2_, bf16[128,1024]{1,0:T(8,128)(2,1)S(1)} %copy-done.1, s32[1,16]{1,0:T(1,128)S(1)} %copy-done.2), custom_call_target="tpu_custom_call" | custom-call | flops 402653184 | bytes 3145728 | tf_op jit(solution)/shard_map/pallas_call | solution.py:137
  19.4 0.0 collective-permute-done.4.refs_5_
  19.4 2.3 %collective-permute-start.8 = (s32[1,16]{1,0:T(1,128)S(1)}, s32[1,16]{1,0:T(1,128)S(1)}, u32[]{:S(2)}, u32[]{:S(2)}) collective-permute-start(s32[1,16]{1,0:T(1,128)S(1)} %collective-permute-done.4.refs_5_), channel_id=1, source_target_pairs={{0,5},{1,2},{2,1},{3,6},{4,9},{5,0},{6,3},{7,10},{8,13},{9,4},{10,... | collective-permute-start | bytes 200 | tf_op jit(solution)/shard_map/ppermute | solution.py:167
  21.7 0.0 collective-permute-done.5.refs_6_
  21.7 0.6 %collective-permute-start.9 = (s32[1,16]{1,0:T(1,128)S(1)}, s32[1,16]{1,0:T(1,128)S(1)}, u32[]{:S(2)}, u32[]{:S(2)}) collective-permute-start(s32[1,16]{1,0:T(1,128)S(1)} %collective-permute-done.5.refs_6_), channel_id=1, source_target_pairs={{0,3},{1,4},{2,7},{3,0},{4,1},{5,8},{6,11},{7,2},{8,5},{9,12},{10,... | collective-permute-start | bytes 200 | tf_op jit(solution)/shard_map/ppermute | solution.py:167
  22.3 0.7 %collective-permute-done.8.refs_5_ = s32[1,16]{1,0:T(1,128)S(1)} collective-permute-done((s32[1,16]{1,0:T(1,128)S(1)}, s32[1,16]{1,0:T(1,128)S(1)}, u32[]{:S(2)}, u32[]{:S(2)}) %collective-permute-start.8) | collective-permute-done | bytes 96 | tf_op jit(solution)/shard_map/ppermute | solution.py:167
  23.0 0.9 %collective-permute-start.12 = (s32[1,16]{1,0:T(1,128)S(1)}, s32[1,16]{1,0:T(1,128)S(1)}, u32[]{:S(2)}, u32[]{:S(2)}) collective-permute-start(s32[1,16]{1,0:T(1,128)S(1)} %collective-permute-done.8.refs_5_), channel_id=1, source_target_pairs={{0,3},{1,4},{2,7},{3,0},{4,1},{5,8},{6,11},{7,2},{8,5},{9,12},{10,... | collective-permute-start | bytes 200 | tf_op jit(solution)/shard_map/ppermute | solution.py:167
  23.9 1.1 %shard_map.71 = (f32[8,1536]{1,0:T(8,128)S(1)}, f32[256,128]{1,0:T(8,128)S(1)}) custom-call(bf16[1536,1024]{1,0:T(8,128)(2,1)S(1)} %copy-done, f32[1,1536]{1,0:T(1,128)S(1)} %shard_map.68.refs_1_.refs_2_, f32[8,1536]{1,0:T(8,128)S(1)} %get-tuple-element.23.refs_2_, ...), custom_call_target="tpu_custom_call", output_to_operand_aliasing={{0}: (2, {})} | custom-call | flops 805306368 | bytes 3145728 | tf_op jit(solution)/shard_map/pallas_call | solution.py:137
  25.0 0.1 collective-permute-done.9.refs_6_
  25.1 1.7 %collective-permute-start.1 = (f32[1,1536]{1,0:T(1,128)S(1)}, f32[1,1536]{1,0:T(1,128)S(1)}, u32[]{:S(2)}, u32[]{:S(2)}) collective-permute-start(f32[1,1536]{1,0:T(1,128)S(1)} %shard_map.68.refs_1_.refs_2_), channel_id=1, source_target_pairs={{0,1},{1,0},{2,3},{3,2},{4,5},{5,4},{6,7},{7,6},{8,9},{9,8},{10,11... | collective-permute-start | bytes 18440 | tf_op jit(solution)/shard_map/ppermute | solution.py:167
  26.8 0.0 collective-permute-done.12.refs_8_
  26.8 1.2 %collective-permute-start.13 = (s32[1,16]{1,0:T(1,128)S(1)}, s32[1,16]{1,0:T(1,128)S(1)}, u32[]{:S(2)}, u32[]{:S(2)}) collective-permute-start(s32[1,16]{1,0:T(1,128)S(1)} %collective-permute-done.9.refs_6_), channel_id=1, source_target_pairs={{0,5},{1,2},{2,1},{3,6},{4,9},{5,0},{6,3},{7,10},{8,13},{9,4},{10,... | collective-permute-start | bytes 200 | tf_op jit(solution)/shard_map/ppermute | solution.py:167
  28.0 0.0 collective-permute-done.7.refs_4_
  28.0 0.6 %collective-permute-start.17 = (s32[1,16]{1,0:T(1,128)S(1)}, s32[1,16]{1,0:T(1,128)S(1)}, u32[]{:S(2)}, u32[]{:S(2)}) collective-permute-start(s32[1,16]{1,0:T(1,128)S(1)} %collective-permute-done.12.refs_8_), channel_id=1, source_target_pairs={{0,5},{1,2},{2,1},{3,6},{4,9},{5,0},{6,3},{7,10},{8,13},{9,4},{10,... | collective-permute-start | bytes 200 | tf_op jit(solution)/shard_map/ppermute | solution.py:167
  28.6 1.1 %shard_map.73 = (f32[8,1536]{1,0:T(8,128)S(1)}, f32[256,128]{1,0:T(8,128)S(1)}) custom-call(bf16[1536,1024]{1,0:T(8,128)(2,1)S(1)} %copy-done, f32[1,1536]{1,0:T(1,128)S(1)} %shard_map.68.refs_1_.refs_2_, f32[8,1536]{1,0:T(8,128)S(1)} %get-tuple-element.26.refs_2_, ...), custom_call_target="tpu_custom_call", output_to_operand_aliasing={{0}: (2, {})} | custom-call | flops 805306368 | bytes 3145728 | tf_op jit(solution)/shard_map/pallas_call | solution.py:137
  29.7 0.0 collective-permute-done.1.refs_1_.refs_3_
  29.7 1.3 %collective-permute-start.11 = (bf16[128,1024]{1,0:T(8,128)(2,1)S(1)}, bf16[128,1024]{1,0:T(8,128)(2,1)S(1)}, u32[]{:S(2)}, u32[]{:S(2)}) collective-permute-start(bf16[128,1024]{1,0:T(8,128)(2,1)S(1)} %collective-permute-done.7.refs_4_), channel_id=1, source_target_pairs={{0,5},{1,2},{2,1},{3,6},{4,9},{5,0},{6,3},{7,10},{8,13},{9,4},{10,... | collective-permute-start | bytes 786440 | tf_op jit(solution)/shard_map/ppermute | solution.py:167
  31.0 0.0 collective-permute-done.10.refs_6_
  31.0 0.6 %collective-permute-start.16 = (bf16[128,1024]{1,0:T(8,128)(2,1)S(1)}, bf16[128,1024]{1,0:T(8,128)(2,1)S(1)}, u32[]{:S(2)}, u32[]{:S(2)}) collective-permute-start(bf16[128,1024]{1,0:T(8,128)(2,1)S(1)} %collective-permute-done.10.refs_6_), channel_id=1, source_target_pairs={{0,5},{1,2},{2,1},{3,6},{4,9},{5,0},{6,3},{7,10},{8,13},{9,4},{10,... | collective-permute-start | bytes 786440 | tf_op jit(solution)/shard_map/ppermute | solution.py:167
  31.5 0.0 collective-permute-done.refs_0_.refs_1_
  31.5 1.3 %shard_map.70 = (f32[8,1536]{1,0:T(8,128)S(1)}, f32[1,128]{1,0:T(1,128)S(1)}) custom-call(bf16[1536,1024]{1,0:T(8,128)(2,1)S(1)} %collective-permute-done.refs_0_.refs_1_, f32[1,1536]{1,0:T(1,128)S(1)} %collective-permute-done.1.refs_1_.refs_3_, bf16[128,1024]{1,0:T(8,128)(2,1)S(1)} %copy-done.1, s32[1,16]{1,0:T(1,128)S(1)} %copy-done.2, ...), custom_call_target="tpu_custom_call" | custom-call | flops 402653184 | bytes 3145728 | tf_op jit(solution)/shard_map/pallas_call | solution.py:137
  32.8 1.2 %shard_map.72 = (f32[8,1536]{1,0:T(8,128)S(1)}, f32[2,128]{1,0:T(2,128)S(1)}) custom-call(bf16[1536,1024]{1,0:T(8,128)(2,1)S(1)} %collective-permute-done.refs_0_.refs_1_, f32[1,1536]{1,0:T(1,128)S(1)} %collective-permute-done.1.refs_1_.refs_3_, f32[8,1536]{1,0:T(8,128)S(1)} %get-tuple-element.22.refs_2_, ...), custom_call_target="tpu_custom_call", output_to_operand_aliasing={{0}: (2, {})} | custom-call | flops 805306368 | bytes 3145728 | tf_op jit(solution)/shard_map/pallas_call | solution.py:137
  34.0 1.2 %shard_map.74 = (f32[8,1536]{1,0:T(8,128)S(1)}, f32[2,128]{1,0:T(2,128)S(1)}) custom-call(bf16[1536,1024]{1,0:T(8,128)(2,1)S(1)} %collective-permute-done.refs_0_.refs_1_, f32[1,1536]{1,0:T(1,128)S(1)} %collective-permute-done.1.refs_1_.refs_3_, f32[8,1536]{1,0:T(8,128)S(1)} %get-tuple-element.28.refs_2_, ...), custom_call_target="tpu_custom_call", output_to_operand_aliasing={{0}: (2, {})} | custom-call | flops 805306368 | bytes 3145728 | tf_op jit(solution)/shard_map/pallas_call | solution.py:137
  35.2 0.0 collective-permute-done.13.refs_9_
  35.3 0.3 collective-permute-done.11.refs_7_
  35.6 2.1 %shard_map.75 = (f32[8,1536]{1,0:T(8,128)S(1)}, f32[8,1536]{1,0:T(8,128)S(1)}, f32[2,128]{1,0:T(2,128)S(1)}) custom-call(bf16[1536,1024]{1,0:T(8,128)(2,1)S(1)} %copy-done, bf16[1536,1024]{1,0:T(8,128)(2,1)S(1)} %collective-permute-done.refs_0_.refs_1_, f32[1,1536]{1,0:T(1,128)S(1)} %shard_map.68.refs_1_.refs_2_, ...), custom_call_target="tpu_custom_call", output_to_operand_aliasing={{0}: (4, {}), {1}: (5, {})} | custom-call | flops 1610612736 | bytes 6291456 | tf_op jit(solution)/shard_map/pallas_call | solution.py:137
  37.7 2.5 %collective-permute-start.14 = (f32[4,128]{1,0:T(4,128)S(1)}, f32[4,128]{1,0:T(4,128)S(1)}, u32[]{:S(2)}, u32[]{:S(2)}) collective-permute-start(f32[4,128]{1,0:T(4,128)S(1)} %pad_maximum_fusion), channel_id=1, source_target_pairs={{0,3},{1,4},{2,7},{3,0},{4,1},{5,8},{6,11},{7,2},{8,5},{9,12},{10,... | collective-permute-start | bytes 6152 | tf_op jit(solution)/shard_map/ppermute | solution.py:167
  40.3 0.0 collective-permute-done.17.refs_7_
  40.3 0.0 collective-permute-done.16.refs_6_
  40.3 0.0 copy-start.3
  40.3 2.3 %shard_map.76 = (f32[8,1536]{1,0:T(8,128)S(1)}, f32[8,1536]{1,0:T(8,128)S(1)}, f32[1,128]{1,0:T(1,128)S(1)}) custom-call(bf16[1536,1024]{1,0:T(8,128)(2,1)S(1)} %copy-done, bf16[1536,1024]{1,0:T(8,128)(2,1)S(1)} %collective-permute-done.refs_0_.refs_1_, f32[1,1536]{1,0:T(1,128)S(1)} %shard_map.68.refs_1_.refs_2_, ...), custom_call_target="tpu_custom_call", output_to_operand_aliasing={{0}: (4, {}), {1}: (5, {})} | custom-call | flops 805306368 | bytes 6291456 | tf_op jit(solution)/shard_map/pallas_call | solution.py:137
  42.6 0.0 collective-permute-done.14
  42.6 1.6 %collective-permute-start.15 = (f32[1,128]{1,0:T(1,128)S(1)}, f32[1,128]{1,0:T(1,128)S(1)}, u32[]{:S(2)}, u32[]{:S(2)}) collective-permute-start(f32[1,128]{1,0:T(1,128)S(1)} %get-tuple-element.38), channel_id=1, source_target_pairs={{0,6},{1,9},{2,10},{3,5},{4,2},{5,13},{6,14},{7,1},{8,0},{9,15},{1... | collective-permute-start | bytes 1544 | tf_op jit(solution)/shard_map/ppermute | solution.py:167
  44.2 1.3 %collective-permute-start.18 = (f32[1,128]{1,0:T(1,128)S(1)}, f32[1,128]{1,0:T(1,128)S(1)}, u32[]{:S(2)}, u32[]{:S(2)}) collective-permute-start(f32[1,128]{1,0:T(1,128)S(1)} %get-tuple-element.40), channel_id=1, source_target_pairs={{0,14},{1,15},{2,12},{3,13},{4,10},{5,11},{6,8},{7,9},{8,6},{9,7},... | collective-permute-start | bytes 1544 | tf_op jit(solution)/shard_map/ppermute | solution.py:167
  45.5 1.9 %collective-permute-start.19 = (f32[1,128]{1,0:T(1,128)S(1)}, f32[1,128]{1,0:T(1,128)S(1)}, u32[]{:S(2)}, u32[]{:S(2)}) collective-permute-start(f32[1,128]{1,0:T(1,128)S(1)} %get-tuple-element.39), channel_id=1, source_target_pairs={{0,8},{1,7},{2,4},{3,11},{4,12},{5,3},{6,0},{7,15},{8,14},{9,1},{1... | collective-permute-start | bytes 1544 | tf_op jit(solution)/shard_map/ppermute | solution.py:167
  48.0 0.4 collective-permute-start.20
  48.4 0.0 collective-permute-done.15
  48.5 2.0 %collective-permute-done.18 = f32[1,128]{1,0:T(1,128)S(1)} collective-permute-done((f32[1,128]{1,0:T(1,128)S(1)}, f32[1,128]{1,0:T(1,128)S(1)}, u32[]{:S(2)}, u32[]{:S(2)}) %collective-permute-start.18) | collective-permute-done | bytes 544 | tf_op jit(solution)/shard_map/ppermute | solution.py:167
  50.4 0.0 collective-permute-done.19
  50.5 0.5 %compare_select_fusion = f32[128]{0:T(128)} fusion(f32[1,128]{1,0:T(1,128)S(1)} %collective-permute-done.19, f32[1,128]{1,0:T(1,128)S(1)} %collective-permute-done.18, f32[1,128]{1,0:T(1,128)S(1)} %collective-permute-done.15, f32[1,128]{1,0:T(1,128)S(1)} %get-tuple-element.21, f32[4,128]{1,0:T(4,128)S(1)} %collective-permute-done.14, s32[]{:T(128)} %bitcast.3), kind=kLoop, calls=%fused_computation.2 | loop fusion | flops 896 | bytes 3076 | tf_op jit(solution)/shard_map/jit(_where)/select_n | solution.py:213
  51.0 0.0 collective-permute-done.20
  51.0 0.0 copy-done.3
  51.0 0.6 %multiply_maximum_fusion = f32[1536]{0:T(1024)} fusion(f32[1536]{0:T(1024)S(1)} %copy-done.3, f32[1536]{0:T(1024)S(1)} %reduce_max.18, f32[1536]{0:T(1024)S(1)} %collective-permute-done.20), kind=kLoop, calls=%fused_computation | loop fusion | flops 4608 | bytes 24576 | tf_op jit(solution)/shard_map/max | solution.py:210
  (6 shorter events, 0.1 us)
Async XLA Ops:
  0.6 30.9 %collective-permute-start = (bf16[1536,1024]{1,0:T(8,128)(2,1)}, bf16[1536,1024]{1,0:T(8,128)(2,1)S(1)}, u32[]{:S(2)}, u32[]{:S(2)}) collective-permute-start(bf16[1536,1024]{1,0:T(8,128)(2,1)} %refs_0_.9), channel_id=1, source_target_pairs={{0,1},{1,0},{2,3},{3,2},{4,5},{5,4},{6,7},{7,6},{8,9},{9,8},{10,11... | collective-permute-start | bytes 9437192 | tf_op jit(solution)/shard_map/ppermute | solution.py:167
  1.2 8.6 %collective-permute-start.2 = (bf16[128,1024]{1,0:T(8,128)(2,1)}, bf16[128,1024]{1,0:T(8,128)(2,1)S(1)}, u32[]{:S(2)}, u32[]{:S(2)}) collective-permute-start(bf16[128,1024]{1,0:T(8,128)(2,1)} %refs_2_.3), channel_id=1, source_target_pairs={{0,3},{1,4},{2,7},{3,0},{4,1},{5,8},{6,11},{7,2},{8,5},{9,12},{10,... | collective-permute-start | bytes 786440 | tf_op jit(solution)/shard_map/ppermute | solution.py:167
  3.8 12.5 %collective-permute-start.3 = (bf16[128,1024]{1,0:T(8,128)(2,1)}, bf16[128,1024]{1,0:T(8,128)(2,1)S(1)}, u32[]{:S(2)}, u32[]{:S(2)}) collective-permute-start(bf16[128,1024]{1,0:T(8,128)(2,1)} %refs_2_.3), channel_id=1, source_target_pairs={{0,5},{1,2},{2,1},{3,6},{4,9},{5,0},{6,3},{7,10},{8,13},{9,4},{10,... | collective-permute-start | bytes 786440 | tf_op jit(solution)/shard_map/ppermute | solution.py:167
  9.8 7.0 %collective-permute-start.6 = (bf16[128,1024]{1,0:T(8,128)(2,1)S(1)}, bf16[128,1024]{1,0:T(8,128)(2,1)S(1)}, u32[]{:S(2)}, u32[]{:S(2)}) collective-permute-start(bf16[128,1024]{1,0:T(8,128)(2,1)S(1)} %collective-permute-done.2.refs_3_), channel_id=1, source_target_pairs={{0,5},{1,2},{2,1},{3,6},{4,9},{5,0},{6,3},{7,10},{8,13},{9,4},{10,... | collective-permute-start | bytes 786440 | tf_op jit(solution)/shard_map/ppermute | solution.py:167
  12.4 7.0 %collective-permute-start.4 = (s32[1,16]{1,0:T(1,128)}, s32[1,16]{1,0:T(1,128)S(1)}, u32[]{:S(2)}, u32[]{:S(2)}) collective-permute-start(s32[1,16]{1,0:T(1,128)} %refs_3_.3), channel_id=1, source_target_pairs={{0,3},{1,4},{2,7},{3,0},{4,1},{5,8},{6,11},{7,2},{8,5},{9,12},{10,... | collective-permute-start | bytes 200 | tf_op jit(solution)/shard_map/ppermute | solution.py:167
  12.7 9.0 %collective-permute-start.5 = (s32[1,16]{1,0:T(1,128)}, s32[1,16]{1,0:T(1,128)S(1)}, u32[]{:S(2)}, u32[]{:S(2)}) collective-permute-start(s32[1,16]{1,0:T(1,128)} %refs_3_.3), channel_id=1, source_target_pairs={{0,5},{1,2},{2,1},{3,6},{4,9},{5,0},{6,3},{7,10},{8,13},{9,4},{10,... | collective-permute-start | bytes 200 | tf_op jit(solution)/shard_map/ppermute | solution.py:167
  16.3 1.9 %copy-start = (bf16[1536,1024]{1,0:T(8,128)(2,1)S(1)}, bf16[1536,1024]{1,0:T(8,128)(2,1)}, u32[]{:S(2)}) copy-start(bf16[1536,1024]{1,0:T(8,128)(2,1)} %refs_0_.9) | copy-start | bytes 9437188
  16.3 1.9 %copy-start.1 = (bf16[128,1024]{1,0:T(8,128)(2,1)S(1)}, bf16[128,1024]{1,0:T(8,128)(2,1)}, u32[]{:S(2)}) copy-start(bf16[128,1024]{1,0:T(8,128)(2,1)} %refs_2_.3) | copy-start | bytes 786436
  16.3 1.9 %copy-start.2 = (s32[1,16]{1,0:T(1,128)S(1)}, s32[1,16]{1,0:T(1,128)}, u32[]{:S(2)}) copy-start(s32[1,16]{1,0:T(1,128)} %refs_3_.3) | copy-start | bytes 196
  16.3 11.7 %collective-permute-start.7 = (bf16[128,1024]{1,0:T(8,128)(2,1)S(1)}, bf16[128,1024]{1,0:T(8,128)(2,1)S(1)}, u32[]{:S(2)}, u32[]{:S(2)}) collective-permute-start(bf16[128,1024]{1,0:T(8,128)(2,1)S(1)} %collective-permute-done.3.refs_4_), channel_id=1, source_target_pairs={{0,3},{1,4},{2,7},{3,0},{4,1},{5,8},{6,11},{7,2},{8,5},{9,12},{10,... | collective-permute-start | bytes 786440 | tf_op jit(solution)/shard_map/ppermute | solution.py:167
  16.8 14.1 %collective-permute-start.10 = (bf16[128,1024]{1,0:T(8,128)(2,1)S(1)}, bf16[128,1024]{1,0:T(8,128)(2,1)S(1)}, u32[]{:S(2)}, u32[]{:S(2)}) collective-permute-start(bf16[128,1024]{1,0:T(8,128)(2,1)S(1)} %collective-permute-done.6.refs_3_), channel_id=1, source_target_pairs={{0,3},{1,4},{2,7},{3,0},{4,1},{5,8},{6,11},{7,2},{8,5},{9,12},{10,... | collective-permute-start | bytes 786440 | tf_op jit(solution)/shard_map/ppermute | solution.py:167
  19.4 3.6 %collective-permute-start.8 = (s32[1,16]{1,0:T(1,128)S(1)}, s32[1,16]{1,0:T(1,128)S(1)}, u32[]{:S(2)}, u32[]{:S(2)}) collective-permute-start(s32[1,16]{1,0:T(1,128)S(1)} %collective-permute-done.4.refs_5_), channel_id=1, source_target_pairs={{0,5},{1,2},{2,1},{3,6},{4,9},{5,0},{6,3},{7,10},{8,13},{9,4},{10,... | collective-permute-start | bytes 200 | tf_op jit(solution)/shard_map/ppermute | solution.py:167
  21.7 3.4 %collective-permute-start.9 = (s32[1,16]{1,0:T(1,128)S(1)}, s32[1,16]{1,0:T(1,128)S(1)}, u32[]{:S(2)}, u32[]{:S(2)}) collective-permute-start(s32[1,16]{1,0:T(1,128)S(1)} %collective-permute-done.5.refs_6_), channel_id=1, source_target_pairs={{0,3},{1,4},{2,7},{3,0},{4,1},{5,8},{6,11},{7,2},{8,5},{9,12},{10,... | collective-permute-start | bytes 200 | tf_op jit(solution)/shard_map/ppermute | solution.py:167
  23.0 3.8 %collective-permute-start.12 = (s32[1,16]{1,0:T(1,128)S(1)}, s32[1,16]{1,0:T(1,128)S(1)}, u32[]{:S(2)}, u32[]{:S(2)}) collective-permute-start(s32[1,16]{1,0:T(1,128)S(1)} %collective-permute-done.8.refs_5_), channel_id=1, source_target_pairs={{0,3},{1,4},{2,7},{3,0},{4,1},{5,8},{6,11},{7,2},{8,5},{9,12},{10,... | collective-permute-start | bytes 200 | tf_op jit(solution)/shard_map/ppermute | solution.py:167
  25.1 4.6 %collective-permute-start.1 = (f32[1,1536]{1,0:T(1,128)S(1)}, f32[1,1536]{1,0:T(1,128)S(1)}, u32[]{:S(2)}, u32[]{:S(2)}) collective-permute-start(f32[1,1536]{1,0:T(1,128)S(1)} %shard_map.68.refs_1_.refs_2_), channel_id=1, source_target_pairs={{0,1},{1,0},{2,3},{3,2},{4,5},{5,4},{6,7},{7,6},{8,9},{9,8},{10,11... | collective-permute-start | bytes 18440 | tf_op jit(solution)/shard_map/ppermute | solution.py:167
  26.8 8.5 %collective-permute-start.13 = (s32[1,16]{1,0:T(1,128)S(1)}, s32[1,16]{1,0:T(1,128)S(1)}, u32[]{:S(2)}, u32[]{:S(2)}) collective-permute-start(s32[1,16]{1,0:T(1,128)S(1)} %collective-permute-done.9.refs_6_), channel_id=1, source_target_pairs={{0,5},{1,2},{2,1},{3,6},{4,9},{5,0},{6,3},{7,10},{8,13},{9,4},{10,... | collective-permute-start | bytes 200 | tf_op jit(solution)/shard_map/ppermute | solution.py:167
  28.0 12.3 %collective-permute-start.17 = (s32[1,16]{1,0:T(1,128)S(1)}, s32[1,16]{1,0:T(1,128)S(1)}, u32[]{:S(2)}, u32[]{:S(2)}) collective-permute-start(s32[1,16]{1,0:T(1,128)S(1)} %collective-permute-done.12.refs_8_), channel_id=1, source_target_pairs={{0,5},{1,2},{2,1},{3,6},{4,9},{5,0},{6,3},{7,10},{8,13},{9,4},{10,... | collective-permute-start | bytes 200 | tf_op jit(solution)/shard_map/ppermute | solution.py:167
  29.7 5.9 %collective-permute-start.11 = (bf16[128,1024]{1,0:T(8,128)(2,1)S(1)}, bf16[128,1024]{1,0:T(8,128)(2,1)S(1)}, u32[]{:S(2)}, u32[]{:S(2)}) collective-permute-start(bf16[128,1024]{1,0:T(8,128)(2,1)S(1)} %collective-permute-done.7.refs_4_), channel_id=1, source_target_pairs={{0,5},{1,2},{2,1},{3,6},{4,9},{5,0},{6,3},{7,10},{8,13},{9,4},{10,... | collective-permute-start | bytes 786440 | tf_op jit(solution)/shard_map/ppermute | solution.py:167
  31.0 9.3 %collective-permute-start.16 = (bf16[128,1024]{1,0:T(8,128)(2,1)S(1)}, bf16[128,1024]{1,0:T(8,128)(2,1)S(1)}, u32[]{:S(2)}, u32[]{:S(2)}) collective-permute-start(bf16[128,1024]{1,0:T(8,128)(2,1)S(1)} %collective-permute-done.10.refs_6_), channel_id=1, source_target_pairs={{0,5},{1,2},{2,1},{3,6},{4,9},{5,0},{6,3},{7,10},{8,13},{9,4},{10,... | collective-permute-start | bytes 786440 | tf_op jit(solution)/shard_map/ppermute | solution.py:167
  37.7 4.8 %collective-permute-start.14 = (f32[4,128]{1,0:T(4,128)S(1)}, f32[4,128]{1,0:T(4,128)S(1)}, u32[]{:S(2)}, u32[]{:S(2)}) collective-permute-start(f32[4,128]{1,0:T(4,128)S(1)} %pad_maximum_fusion), channel_id=1, source_target_pairs={{0,3},{1,4},{2,7},{3,0},{4,1},{5,8},{6,11},{7,2},{8,5},{9,12},{10,... | collective-permute-start | bytes 6152 | tf_op jit(solution)/shard_map/ppermute | solution.py:167
  40.3 10.7 %copy-start.3 = (f32[1536]{0:T(1024)S(1)}, f32[1536]{0:T(1024)}, u32[]{:S(2)}) copy-start(f32[1536]{0:T(1024)} %param.6) | copy-start | bytes 18436
  42.6 5.8 %collective-permute-start.15 = (f32[1,128]{1,0:T(1,128)S(1)}, f32[1,128]{1,0:T(1,128)S(1)}, u32[]{:S(2)}, u32[]{:S(2)}) collective-permute-start(f32[1,128]{1,0:T(1,128)S(1)} %get-tuple-element.38), channel_id=1, source_target_pairs={{0,6},{1,9},{2,10},{3,5},{4,2},{5,13},{6,14},{7,1},{8,0},{9,15},{1... | collective-permute-start | bytes 1544 | tf_op jit(solution)/shard_map/ppermute | solution.py:167
  44.2 6.3 %collective-permute-start.18 = (f32[1,128]{1,0:T(1,128)S(1)}, f32[1,128]{1,0:T(1,128)S(1)}, u32[]{:S(2)}, u32[]{:S(2)}) collective-permute-start(f32[1,128]{1,0:T(1,128)S(1)} %get-tuple-element.40), channel_id=1, source_target_pairs={{0,14},{1,15},{2,12},{3,13},{4,10},{5,11},{6,8},{7,9},{8,6},{9,7},... | collective-permute-start | bytes 1544 | tf_op jit(solution)/shard_map/ppermute | solution.py:167
  45.5 5.0 %collective-permute-start.19 = (f32[1,128]{1,0:T(1,128)S(1)}, f32[1,128]{1,0:T(1,128)S(1)}, u32[]{:S(2)}, u32[]{:S(2)}) collective-permute-start(f32[1,128]{1,0:T(1,128)S(1)} %get-tuple-element.39), channel_id=1, source_target_pairs={{0,8},{1,7},{2,4},{3,11},{4,12},{5,3},{6,0},{7,15},{8,14},{9,1},{1... | collective-permute-start | bytes 1544 | tf_op jit(solution)/shard_map/ppermute | solution.py:167
  48.0 2.9 %collective-permute-start.20 = (f32[1536]{0:T(1024)S(1)}, f32[1536]{0:T(1024)S(1)}, u32[]{:S(2)}, u32[]{:S(2)}) collective-permute-start(f32[1536]{0:T(1024)S(1)} %reduce_max.19), channel_id=1, source_target_pairs={{0,1},{1,0},{2,3},{3,2},{4,5},{5,4},{6,7},{7,6},{8,9},{9,8},{10,11... | collective-permute-start | bytes 18440 | tf_op jit(solution)/shard_map/ppermute | solution.py:167

commit v2 on v1

--- a/solution.py
+++ b/solution.py
@@ -41,7 +41,7 @@
 
 def bias_column(picks, slots):
     slot = lax.broadcasted_iota(jnp.int32, (slots, picks.shape[1]), 0)
-    hit = jnp.where(slot == picks, 0.0, -jnp.inf)
+    hit = jnp.where(slot == picks[0:1].astype(jnp.int32), 0.0, -jnp.inf)
     return jnp.max(hit, axis=1, keepdims=True)
 
 
@@ -70,7 +70,7 @@
 
 
 def tile_of(points):
-    return math.gcd(points, 256)
+    return math.gcd(points, 768)
 
 
 def scale_body(root, cov, out):
@@ -150,6 +150,10 @@
     return list(out[:halves]), out[halves]
 
 
+def rider(chips, j):
+    return 6 if j == 0 and chips == 8 else None
+
+
 def per_device(ring, points, coverage, candidates, cand_count, acc_index):
     width = points.shape[1]
     slots = candidates.shape[0]
@@ -172,39 +176,58 @@
     cov = scaled(root, coverage, 32 * slots * points.shape[0] * width)
     pts = [points, swap(points)]
     covs = [cov, swap(cov)]
-    alone = [candidates], [acc_index]
-    run_a, total = score(pts[:1], covs[:1], None, *alone, last=False)
-    run_b, gain = score(pts[1:], covs[1:], None, *alone, before=total)
-    runs = run_a + run_b
-
-    blocks, picks, parts, home = {}, {}, {}, {}
+
+    half = chips // 2
+
+    def step_of(k):
+        return (1 if k % 2 else -1) * sign((k + 1) // 2)
+
+    def sign(hop):
+        return 1 if hop % 2 else -1
+
+    def row_of(tag):
+        return jnp.pad(
+            tag[0:1].astype(F32), ((0, 0), (0, slots - tag.shape[1])), constant_values=-1.0
+        )
+
+    blocks, tags = {0: candidates}, {0: acc_index}
     for k in range(1, chips):
-        hop = (k + 1) // 2
-        step = (1 if k % 2 else -1) * (1 if hop % 2 else -1)
-        home[k] = (step * hop) % chips
-        blocks[k] = move(candidates if k <= 2 else blocks[k - 2], step, 1)
-        picks[k] = move(acc_index if k <= 2 else picks[k - 2], step, 1)
-    for k in range(2, chips + 1, 2):
-        ks = [j for j in (k - 1, k) if j < chips]
-        group = [blocks[j] for j in ks], [picks[j] for j in ks]
-        if k < chips - 2:
-            run_a, total = score(pts[:1], covs[:1], runs[:1], *group, last=False)
-            run_b, sums = score(pts[1:], covs[1:], runs[1:], *group, before=total)
+        blocks[k] = move(blocks[max(k - 2, 0)], step_of(k), 1)
+    riders = {rider(chips, j): j for j in range(half - 1)}
+    for k in range(1, chips):
+        if k not in riders:
+            tags[k] = move(tags[max(k - 2, 0)], step_of(k), 1)
+    runs = None
+    seen = {}
+    for j in range(half):
+        ks = [2 * j, 2 * j + 1]
+        group = [blocks[k] for k in ks], [tags[k] for k in ks]
+        if j < half - 2:
+            near, far = (None, None) if runs is None else (runs[:1], runs[1:])
+            run_a, total = score(pts[:1], covs[:1], near, *group, last=False)
+            run_b, sums = score(pts[1:], covs[1:], far, *group, before=total)
             runs = run_a + run_b
         else:
             runs, sums = score(pts, covs, runs, *group)
-        parts.update({home[j]: sums[row : row + 1] for row, j in enumerate(ks)})
-    odd = [e for e in sorted(parts) if e % 2]
-    came = move(jnp.concatenate([parts[e] for e in odd], axis=0), 1, 1)
-    for row, e in enumerate(odd):
-        to = (1 - e) % chips
-        if to:
-            parts[to] = parts[to] + came[row : row + 1]
+        if j == 0:
+            gain, rows = sums[0:1], [sums[1:2]]
         else:
-            gain = gain + came[row : row + 1]
-    for e in sorted(parts):
-        if e and e % 2 == 0:
-            gain = gain + move(parts[e], e, 0)
+            rows = [sums[1:2] + seen[j - 1][-1], sums[0:1]]
+            if j > 1:
+                rows[1] = rows[1] + seen[j - 1][-2]
+            rows.reverse()
+        if j < half - 1:
+            k = rider(chips, j)
+            lead = []
+            if k is not None:
+                tag, rows[0] = lax.optimization_barrier((tags[k - 2], rows[0]))
+                lead = [row_of(tag)]
+            came = move(jnp.concatenate(lead + rows, axis=0), sign(j + 2), 1)
+            if k is not None:
+                tags[k] = came
+            seen[j] = [came[r : r + 1] for r in range(came.shape[0])]
+    gain = gain + move(rows[1], half, half % 2)
+    gain = gain + move(rows[0], step_of(chips - 2) * (half - 1), (half - 1) % 2)
     other = swap(jnp.max(runs[1], axis=0))
     best = jnp.maximum(jnp.max(runs[0], axis=0), other)
     new_coverage = jnp.maximum(coverage, best / root)

time: 51.8 us -> 53.7 us (1.037)
  waiting for transfers between devices: 7.81 us -> 12.9 us
  Pallas kernels: 11.6 us -> 8.97 us
    ppermute x21, waiting for transfers between devices: 7.81 us -> 12.9 us  [move(): return lax.ppermute(x, 'blk', pairs)]
    pallas_call x8 -> x6, Pallas kernels: 11.6 us -> 8.97 us  [score(): pl.pallas_call(functools.partial(score_body, halves, blocks, fresh, len(c...]
  transfers between devices with their start and end apart: 21 -> 21, of which waited for: 5 -> 5; matrix products, arithmetic and copies ran while one was open for 2% -> 2% of each run, Pallas kernels for 23% -> 17%
where the time goes in v2:
time: 53.7 us; the launch traced here: 53.5 us
  starting transfers between devices  28.3 us (53%)
  waiting for transfers between devices  12.9 us (24%)
  Pallas kernels  8.97 us (17%)
  between operations  1.44 us (3%)
  other arithmetic  1.21 us (2%)
  local copies, waits for them, and re-layouts  0.73 us (1%)
    ppermute x21, starting transfers between devices, move(): return lax.ppermute(x, 'blk', pairs)  28.3 us
    ppermute x21, waiting for transfers between devices, move(): return lax.ppermute(x, 'blk', pairs)  12.9 us
    pallas_call x6, Pallas kernels, score(): pl.pallas_call(functools.partial(score_body, halves, blocks, fresh, len(c...  8.97 us
  transfers between devices with their start and end apart: 21, of which 5 were waited for; matrix products, arithmetic and copies ran while one was open for 2% of the time, Pallas kernels for 17%

profile of v2, /device:TPU:0, one launch (start us, length us, event | category | flops | bytes accessed | tf_op | source)
XLA Modules:
  0.0 53.5 jit_solution(15865593768329718346)
XLA Ops:
  0.6 0.6 %collective-permute-start = (bf16[1536,1024]{1,0:T(8,128)(2,1)}, bf16[1536,1024]{1,0:T(8,128)(2,1)S(1)}, u32[]{:S(2)}, u32[]{:S(2)}) collective-permute-start(bf16[1536,1024]{1,0:T(8,128)(2,1)} %refs_0_.7), channel_id=1, source_target_pairs={{0,1},{1,0},{2,3},{3,2},{4,5},{5,4},{6,7},{7,6},{8,9},{9,8},{10,11... | collective-permute-start | bytes 9437192 | tf_op jit(solution)/shard_map/ppermute | solution.py:171
  1.2 2.6 %collective-permute-start.2 = (bf16[128,1024]{1,0:T(8,128)(2,1)}, bf16[128,1024]{1,0:T(8,128)(2,1)S(1)}, u32[]{:S(2)}, u32[]{:S(2)}) collective-permute-start(bf16[128,1024]{1,0:T(8,128)(2,1)} %refs_2_.3), channel_id=1, source_target_pairs={{0,3},{1,4},{2,7},{3,0},{4,1},{5,8},{6,11},{7,2},{8,5},{9,12},{10,... | collective-permute-start | bytes 786440 | tf_op jit(solution)/shard_map/ppermute | solution.py:171
  3.8 1.3 %collective-permute-start.4 = (bf16[128,1024]{1,0:T(8,128)(2,1)}, bf16[128,1024]{1,0:T(8,128)(2,1)S(1)}, u32[]{:S(2)}, u32[]{:S(2)}) collective-permute-start(bf16[128,1024]{1,0:T(8,128)(2,1)} %refs_2_.3), channel_id=1, source_target_pairs={{0,5},{1,2},{2,1},{3,6},{4,9},{5,0},{6,3},{7,10},{8,13},{9,4},{10,... | collective-permute-start | bytes 786440 | tf_op jit(solution)/shard_map/ppermute | solution.py:171
  5.1 4.7 %collective-permute-done.2.refs_3_ = bf16[128,1024]{1,0:T(8,128)(2,1)S(1)} collective-permute-done((bf16[128,1024]{1,0:T(8,128)(2,1)}, bf16[128,1024]{1,0:T(8,128)(2,1)S(1)}, u32[]{:S(2)}, u32[]{:S(2)}) %collective-permute-start.2) | collective-permute-done | bytes 262176 | tf_op jit(solution)/shard_map/ppermute | solution.py:171
  9.8 2.6 %collective-permute-start.5 = (bf16[128,1024]{1,0:T(8,128)(2,1)S(1)}, bf16[128,1024]{1,0:T(8,128)(2,1)S(1)}, u32[]{:S(2)}, u32[]{:S(2)}) collective-permute-start(bf16[128,1024]{1,0:T(8,128)(2,1)S(1)} %collective-permute-done.2.refs_3_), channel_id=1, source_target_pairs={{0,5},{1,2},{2,1},{3,6},{4,9},{5,0},{6,3},{7,10},{8,13},{9,4},{10,... | collective-permute-start | bytes 786440 | tf_op jit(solution)/shard_map/ppermute | solution.py:171
  12.4 0.3 collective-permute-start.3
  12.7 2.9 %collective-permute-start.6 = (s32[1,16]{1,0:T(1,128)}, s32[1,16]{1,0:T(1,128)S(1)}, u32[]{:S(2)}, u32[]{:S(2)}) collective-permute-start(s32[1,16]{1,0:T(1,128)} %refs_4_.3), channel_id=1, source_target_pairs={{0,5},{1,2},{2,1},{3,6},{4,9},{5,0},{6,3},{7,10},{8,13},{9,4},{10,... | collective-permute-start | bytes 200 | tf_op jit(solution)/shard_map/ppermute | solution.py:171
  15.6 0.7 %broadcast_in_dim.7.cov = f32[1,1536]{1,0:T(1,128)S(1)} reshape(f32[1536]{0:T(1024)} %param.6) | data formatting | bytes 12288 | tf_op jit(solution)/shard_map/broadcast_in_dim | solution.py:88
  16.3 0.0 copy-start
  16.3 0.0 copy-start.1
  16.3 0.0 copy-start.2
  16.3 0.0 collective-permute-done.4.refs_3_
  16.3 0.5 collective-permute-start.8
  16.8 0.0 collective-permute-done.5.refs_4_
  16.8 1.3 %collective-permute-start.9 = (bf16[128,1024]{1,0:T(8,128)(2,1)S(1)}, bf16[128,1024]{1,0:T(8,128)(2,1)S(1)}, u32[]{:S(2)}, u32[]{:S(2)}) collective-permute-start(bf16[128,1024]{1,0:T(8,128)(2,1)S(1)} %collective-permute-done.5.refs_4_), channel_id=1, source_target_pairs={{0,3},{1,4},{2,7},{3,0},{4,1},{5,8},{6,11},{7,2},{8,5},{9,12},{10,... | collective-permute-start | bytes 786440 | tf_op jit(solution)/shard_map/ppermute | solution.py:171
  18.1 0.0 collective-permute-done.3.refs_5_
  18.1 2.3 %collective-permute-start.7 = (s32[1,16]{1,0:T(1,128)S(1)}, s32[1,16]{1,0:T(1,128)S(1)}, u32[]{:S(2)}, u32[]{:S(2)}) collective-permute-start(s32[1,16]{1,0:T(1,128)S(1)} %collective-permute-done.3.refs_5_), channel_id=1, source_target_pairs={{0,5},{1,2},{2,1},{3,6},{4,9},{5,0},{6,3},{7,10},{8,13},{9,4},{10,... | collective-permute-start | bytes 200 | tf_op jit(solution)/shard_map/ppermute | solution.py:171
  20.4 0.0 copy-done
  20.4 0.0 copy-done.1
  20.4 0.0 copy-done.2
  20.4 1.1 %shard_map.69 = (f32[8,1536]{1,0:T(8,128)S(1)}, f32[256,128]{1,0:T(8,128)S(1)}) custom-call(bf16[1536,1024]{1,0:T(8,128)(2,1)S(1)} %copy-done, f32[1,1536]{1,0:T(1,128)S(1)} %shard_map.68.refs_1_.refs_2_, bf16[128,1024]{1,0:T(8,128)(2,1)S(1)} %copy-done.1, bf16[128,1024]{1,0:T(8,128)(2,1)S(1)} %collective-permute-done.2.refs_3_, s32[1,16]{1,0:T(1,128)S(1)} %copy-done.2, ...), custom_call_target="tpu_custom_call" | custom-call | flops 805306368 | bytes 3145728 | tf_op jit(solution)/shard_map/pallas_call | solution.py:137
  21.6 0.0 collective-permute-done.6.refs_5_
  21.6 0.1 collective-permute-start.1
  21.7 0.1 collective-permute-done.7.refs_6_
  21.7 0.9 %collective-permute-start.11 = (s32[1,16]{1,0:T(1,128)S(1)}, s32[1,16]{1,0:T(1,128)S(1)}, u32[]{:S(2)}, u32[]{:S(2)}) collective-permute-start(s32[1,16]{1,0:T(1,128)S(1)} %collective-permute-done.7.refs_6_), channel_id=1, source_target_pairs={{0,3},{1,4},{2,7},{3,0},{4,1},{5,8},{6,11},{7,2},{8,5},{9,12},{10,... | collective-permute-start | bytes 200 | tf_op jit(solution)/shard_map/ppermute | solution.py:171
  22.6 1.1 %shard_map.71 = (f32[8,1536]{1,0:T(8,128)S(1)}, f32[256,128]{1,0:T(8,128)S(1)}) custom-call(bf16[1536,1024]{1,0:T(8,128)(2,1)S(1)} %copy-done, f32[1,1536]{1,0:T(1,128)S(1)} %shard_map.68.refs_1_.refs_2_, f32[8,1536]{1,0:T(8,128)S(1)} %get-tuple-element.20.refs_2_, ...), custom_call_target="tpu_custom_call", output_to_operand_aliasing={{0}: (2, {})} | custom-call | flops 805306368 | bytes 3145728 | tf_op jit(solution)/shard_map/pallas_call | solution.py:137
  23.7 1.4 %collective-permute-done.11.refs_9_ = s32[1,16]{1,0:T(1,128)S(1)} collective-permute-done((s32[1,16]{1,0:T(1,128)S(1)}, s32[1,16]{1,0:T(1,128)S(1)}, u32[]{:S(2)}, u32[]{:S(2)}) %collective-permute-start.11) | collective-permute-done | bytes 96 | tf_op jit(solution)/shard_map/ppermute | solution.py:171
  25.1 0.5 collective-permute-start.10
  25.6 0.0 collective-permute-done.1.refs_1_.refs_3_
  25.6 1.7 %collective-permute-start.15 = (s32[1,16]{1,0:T(1,128)S(1)}, s32[1,16]{1,0:T(1,128)S(1)}, u32[]{:S(2)}, u32[]{:S(2)}) collective-permute-start(s32[1,16]{1,0:T(1,128)S(1)} %collective-permute-done.11.refs_9_), channel_id=1, source_target_pairs={{0,5},{1,2},{2,1},{3,6},{4,9},{5,0},{6,3},{7,10},{8,13},{9,4},{10,... | collective-permute-start | bytes 200 | tf_op jit(solution)/shard_map/ppermute | solution.py:171
  27.3 0.0 collective-permute-done.8.refs_6_
  27.3 0.1 collective-permute-start.12
  27.3 0.0 collective-permute-done.9.refs_7_
  27.4 1.7 %collective-permute-start.13 = (bf16[128,1024]{1,0:T(8,128)(2,1)S(1)}, bf16[128,1024]{1,0:T(8,128)(2,1)S(1)}, u32[]{:S(2)}, u32[]{:S(2)}) collective-permute-start(bf16[128,1024]{1,0:T(8,128)(2,1)S(1)} %collective-permute-done.9.refs_7_), channel_id=1, source_target_pairs={{0,5},{1,2},{2,1},{3,6},{4,9},{5,0},{6,3},{7,10},{8,13},{9,4},{10,... | collective-permute-start | bytes 786440 | tf_op jit(solution)/shard_map/ppermute | solution.py:171
  29.0 0.0 collective-permute-done.refs_0_.refs_1_
  29.0 1.2 %shard_map.70 = (f32[8,1536]{1,0:T(8,128)S(1)}, f32[2,128]{1,0:T(2,128)S(1)}) custom-call(bf16[1536,1024]{1,0:T(8,128)(2,1)S(1)} %collective-permute-done.refs_0_.refs_1_, f32[1,1536]{1,0:T(1,128)S(1)} %collective-permute-done.1.refs_1_.refs_3_, bf16[128,1024]{1,0:T(8,128)(2,1)S(1)} %copy-done.1, bf16[128,1024]{1,0:T(8,128)(2,1)S(1)} %collective-permute-done.2.refs_3_, ...), custom_call_target="tpu_custom_call" | custom-call | flops 805306368 | bytes 3145728 | tf_op jit(solution)/shard_map/pallas_call | solution.py:137
  30.3 0.0 collective-permute-done.10.refs_8_
  30.3 0.1 collective-permute-start.14
  30.4 1.2 %shard_map.72 = (f32[8,1536]{1,0:T(8,128)S(1)}, f32[2,128]{1,0:T(2,128)S(1)}) custom-call(bf16[1536,1024]{1,0:T(8,128)(2,1)S(1)} %collective-permute-done.refs_0_.refs_1_, f32[1,1536]{1,0:T(1,128)S(1)} %collective-permute-done.1.refs_1_.refs_3_, f32[8,1536]{1,0:T(8,128)S(1)} %get-tuple-element.22.refs_2_, ...), custom_call_target="tpu_custom_call", output_to_operand_aliasing={{0}: (2, {})} | custom-call | flops 805306368 | bytes 3145728 | tf_op jit(solution)/shard_map/pallas_call | solution.py:137
  31.6 4.3 %collective-permute-done.14.refs_8_ = f32[2,128]{1,0:T(2,128)S(1)} collective-permute-done((f32[2,128]{1,0:T(2,128)S(1)}, f32[2,128]{1,0:T(2,128)S(1)}, u32[]{:S(2)}, u32[]{:S(2)}) %collective-permute-start.14) | collective-permute-done | bytes 1056 | tf_op jit(solution)/shard_map/ppermute | solution.py:171
  36.0 2.2 %collective-permute-start.16 = (f32[2,128]{1,0:T(2,128)S(1)}, f32[2,128]{1,0:T(2,128)S(1)}, u32[]{:S(2)}, u32[]{:S(2)}) collective-permute-start(f32[2,128]{1,0:T(2,128)S(1)} %pad_maximum_fusion), channel_id=1, source_target_pairs={{0,3},{1,4},{2,7},{3,0},{4,1},{5,8},{6,11},{7,2},{8,5},{9,12},{10,... | collective-permute-start | bytes 3080 | tf_op jit(solution)/shard_map/ppermute | solution.py:171
  38.2 2.1 %shard_map.73 = (f32[8,1536]{1,0:T(8,128)S(1)}, f32[8,1536]{1,0:T(8,128)S(1)}, f32[2,128]{1,0:T(2,128)S(1)}) custom-call(bf16[1536,1024]{1,0:T(8,128)(2,1)S(1)} %copy-done, bf16[1536,1024]{1,0:T(8,128)(2,1)S(1)} %collective-permute-done.refs_0_.refs_1_, f32[1,1536]{1,0:T(1,128)S(1)} %shard_map.68.refs_1_.refs_2_, ...), custom_call_target="tpu_custom_call", output_to_operand_aliasing={{0}: (4, {}), {1}: (5, {})} | custom-call | flops 1610612736 | bytes 6291456 | tf_op jit(solution)/shard_map/pallas_call | solution.py:137
  40.4 0.0 collective-permute-done.16
  40.4 1.0 %collective-permute-start.17 = (f32[2,128]{1,0:T(2,128)S(1)}, f32[2,128]{1,0:T(2,128)S(1)}, u32[]{:S(2)}, u32[]{:S(2)}) collective-permute-start(f32[2,128]{1,0:T(2,128)S(1)} %pad_maximum_fusion.1), channel_id=1, source_target_pairs={{0,5},{1,2},{2,1},{3,6},{4,9},{5,0},{6,3},{7,10},{8,13},{9,4},{10,... | collective-permute-start | bytes 3080 | tf_op jit(solution)/shard_map/ppermute | solution.py:171
  41.4 0.0 collective-permute-done.15.refs_9_
  41.4 0.0 collective-permute-done.12.refs_6_
  41.4 0.0 collective-permute-done.13.refs_7_
  41.4 0.0 copy-start.3
  41.4 2.1 %shard_map.74 = (f32[8,1536]{1,0:T(8,128)S(1)}, f32[8,1536]{1,0:T(8,128)S(1)}, f32[2,128]{1,0:T(2,128)S(1)}) custom-call(bf16[1536,1024]{1,0:T(8,128)(2,1)S(1)} %copy-done, bf16[1536,1024]{1,0:T(8,128)(2,1)S(1)} %collective-permute-done.refs_0_.refs_1_, f32[1,1536]{1,0:T(1,128)S(1)} %shard_map.68.refs_1_.refs_2_, ...), custom_call_target="tpu_custom_call", output_to_operand_aliasing={{0}: (4, {}), {1}: (5, {})} | custom-call | flops 1610612736 | bytes 6291456 | tf_op jit(solution)/shard_map/pallas_call | solution.py:137
  43.5 0.0 collective-permute-done.17
  43.5 2.5 %collective-permute-start.19 = (f32[1,128]{1,0:T(1,128)S(1)}, f32[1,128]{1,0:T(1,128)S(1)}, u32[]{:S(2)}, u32[]{:S(2)}) collective-permute-start(f32[1,128]{1,0:T(1,128)S(1)} %get-tuple-element.35), channel_id=1, source_target_pairs={{0,13},{1,10},{2,9},{3,14},{4,15},{5,6},{6,5},{7,12},{8,11},{9,2},... | collective-permute-start | bytes 1544 | tf_op jit(solution)/shard_map/ppermute | solution.py:171
  46.1 1.7 %collective-permute-start.18 = (f32[1,128]{1,0:T(1,128)S(1)}, f32[1,128]{1,0:T(1,128)S(1)}, u32[]{:S(2)}, u32[]{:S(2)}) collective-permute-start(f32[1,128]{1,0:T(1,128)S(1)} %get-tuple-element.34), channel_id=1, source_target_pairs={{0,14},{1,15},{2,12},{3,13},{4,10},{5,11},{6,8},{7,9},{8,6},{9,7},... | collective-permute-start | bytes 1544 | tf_op jit(solution)/shard_map/ppermute | solution.py:171
  48.5 1.5 %collective-permute-start.20 = (f32[1536]{0:T(1024)S(1)}, f32[1536]{0:T(1024)S(1)}, u32[]{:S(2)}, u32[]{:S(2)}) collective-permute-start(f32[1536]{0:T(1024)S(1)} %reduce_max.19), channel_id=1, source_target_pairs={{0,1},{1,0},{2,3},{3,2},{4,5},{5,4},{6,7},{7,6},{8,9},{9,8},{10,11... | collective-permute-start | bytes 18440 | tf_op jit(solution)/shard_map/ppermute | solution.py:171
  49.9 0.0 collective-permute-done.19
  50.0 2.4 %collective-permute-done.18 = f32[1,128]{1,0:T(1,128)S(1)} collective-permute-done((f32[1,128]{1,0:T(1,128)S(1)}, f32[1,128]{1,0:T(1,128)S(1)}, u32[]{:S(2)}, u32[]{:S(2)}) %collective-permute-start.18) | collective-permute-done | bytes 544 | tf_op jit(solution)/shard_map/ppermute | solution.py:171
  52.4 0.5 compare_select_fusion.1
  52.9 0.0 collective-permute-done.20
  52.9 0.0 copy-done.3
  52.9 0.6 %multiply_maximum_fusion = f32[1536]{0:T(1024)} fusion(f32[1536]{0:T(1024)S(1)} %copy-done.3, f32[1536]{0:T(1024)S(1)} %reduce_max.18, f32[1536]{0:T(1024)S(1)} %collective-permute-done.20), kind=kLoop, calls=%fused_computation | loop fusion | flops 4608 | bytes 24576 | tf_op jit(solution)/shard_map/max | solution.py:233
  (11 shorter events, 0.1 us)
Async XLA Ops:
  0.6 28.4 %collective-permute-start = (bf16[1536,1024]{1,0:T(8,128)(2,1)}, bf16[1536,1024]{1,0:T(8,128)(2,1)S(1)}, u32[]{:S(2)}, u32[]{:S(2)}) collective-permute-start(bf16[1536,1024]{1,0:T(8,128)(2,1)} %refs_0_.7), channel_id=1, source_target_pairs={{0,1},{1,0},{2,3},{3,2},{4,5},{5,4},{6,7},{7,6},{8,9},{9,8},{10,11... | collective-permute-start | bytes 9437192 | tf_op jit(solution)/shard_map/ppermute | solution.py:171
  1.2 8.6 %collective-permute-start.2 = (bf16[128,1024]{1,0:T(8,128)(2,1)}, bf16[128,1024]{1,0:T(8,128)(2,1)S(1)}, u32[]{:S(2)}, u32[]{:S(2)}) collective-permute-start(bf16[128,1024]{1,0:T(8,128)(2,1)} %refs_2_.3), channel_id=1, source_target_pairs={{0,3},{1,4},{2,7},{3,0},{4,1},{5,8},{6,11},{7,2},{8,5},{9,12},{10,... | collective-permute-start | bytes 786440 | tf_op jit(solution)/shard_map/ppermute | solution.py:171
  3.8 12.5 %collective-permute-start.4 = (bf16[128,1024]{1,0:T(8,128)(2,1)}, bf16[128,1024]{1,0:T(8,128)(2,1)S(1)}, u32[]{:S(2)}, u32[]{:S(2)}) collective-permute-start(bf16[128,1024]{1,0:T(8,128)(2,1)} %refs_2_.3), channel_id=1, source_target_pairs={{0,5},{1,2},{2,1},{3,6},{4,9},{5,0},{6,3},{7,10},{8,13},{9,4},{10,... | collective-permute-start | bytes 786440 | tf_op jit(solution)/shard_map/ppermute | solution.py:171
  9.8 7.0 %collective-permute-start.5 = (bf16[128,1024]{1,0:T(8,128)(2,1)S(1)}, bf16[128,1024]{1,0:T(8,128)(2,1)S(1)}, u32[]{:S(2)}, u32[]{:S(2)}) collective-permute-start(bf16[128,1024]{1,0:T(8,128)(2,1)S(1)} %collective-permute-done.2.refs_3_), channel_id=1, source_target_pairs={{0,5},{1,2},{2,1},{3,6},{4,9},{5,0},{6,3},{7,10},{8,13},{9,4},{10,... | collective-permute-start | bytes 786440 | tf_op jit(solution)/shard_map/ppermute | solution.py:171
  12.4 5.7 %collective-permute-start.3 = (s32[1,16]{1,0:T(1,128)}, s32[1,16]{1,0:T(1,128)S(1)}, u32[]{:S(2)}, u32[]{:S(2)}) collective-permute-start(s32[1,16]{1,0:T(1,128)} %refs_4_.3), channel_id=1, source_target_pairs={{0,3},{1,4},{2,7},{3,0},{4,1},{5,8},{6,11},{7,2},{8,5},{9,12},{10,... | collective-permute-start | bytes 200 | tf_op jit(solution)/shard_map/ppermute | solution.py:171
  12.7 8.9 %collective-permute-start.6 = (s32[1,16]{1,0:T(1,128)}, s32[1,16]{1,0:T(1,128)S(1)}, u32[]{:S(2)}, u32[]{:S(2)}) collective-permute-start(s32[1,16]{1,0:T(1,128)} %refs_4_.3), channel_id=1, source_target_pairs={{0,5},{1,2},{2,1},{3,6},{4,9},{5,0},{6,3},{7,10},{8,13},{9,4},{10,... | collective-permute-start | bytes 200 | tf_op jit(solution)/shard_map/ppermute | solution.py:171
  16.3 4.1 %copy-start = (bf16[1536,1024]{1,0:T(8,128)(2,1)S(1)}, bf16[1536,1024]{1,0:T(8,128)(2,1)}, u32[]{:S(2)}) copy-start(bf16[1536,1024]{1,0:T(8,128)(2,1)} %refs_0_.7) | copy-start | bytes 9437188
  16.3 4.1 %copy-start.1 = (bf16[128,1024]{1,0:T(8,128)(2,1)S(1)}, bf16[128,1024]{1,0:T(8,128)(2,1)}, u32[]{:S(2)}) copy-start(bf16[128,1024]{1,0:T(8,128)(2,1)} %refs_2_.3) | copy-start | bytes 786436
  16.3 4.1 %copy-start.2 = (s32[1,16]{1,0:T(1,128)S(1)}, s32[1,16]{1,0:T(1,128)}, u32[]{:S(2)}) copy-start(s32[1,16]{1,0:T(1,128)} %refs_4_.3) | copy-start | bytes 196
  16.3 11.0 %collective-permute-start.8 = (bf16[128,1024]{1,0:T(8,128)(2,1)S(1)}, bf16[128,1024]{1,0:T(8,128)(2,1)S(1)}, u32[]{:S(2)}, u32[]{:S(2)}) collective-permute-start(bf16[128,1024]{1,0:T(8,128)(2,1)S(1)} %collective-permute-done.4.refs_3_), channel_id=1, source_target_pairs={{0,3},{1,4},{2,7},{3,0},{4,1},{5,8},{6,11},{7,2},{8,5},{9,12},{10,... | collective-permute-start | bytes 786440 | tf_op jit(solution)/shard_map/ppermute | solution.py:171
  16.8 10.5 %collective-permute-start.9 = (bf16[128,1024]{1,0:T(8,128)(2,1)S(1)}, bf16[128,1024]{1,0:T(8,128)(2,1)S(1)}, u32[]{:S(2)}, u32[]{:S(2)}) collective-permute-start(bf16[128,1024]{1,0:T(8,128)(2,1)S(1)} %collective-permute-done.5.refs_4_), channel_id=1, source_target_pairs={{0,3},{1,4},{2,7},{3,0},{4,1},{5,8},{6,11},{7,2},{8,5},{9,12},{10,... | collective-permute-start | bytes 786440 | tf_op jit(solution)/shard_map/ppermute | solution.py:171
  18.1 3.6 %collective-permute-start.7 = (s32[1,16]{1,0:T(1,128)S(1)}, s32[1,16]{1,0:T(1,128)S(1)}, u32[]{:S(2)}, u32[]{:S(2)}) collective-permute-start(s32[1,16]{1,0:T(1,128)S(1)} %collective-permute-done.3.refs_5_), channel_id=1, source_target_pairs={{0,5},{1,2},{2,1},{3,6},{4,9},{5,0},{6,3},{7,10},{8,13},{9,4},{10,... | collective-permute-start | bytes 200 | tf_op jit(solution)/shard_map/ppermute | solution.py:171
  21.6 4.0 %collective-permute-start.1 = (f32[1,1536]{1,0:T(1,128)S(1)}, f32[1,1536]{1,0:T(1,128)S(1)}, u32[]{:S(2)}, u32[]{:S(2)}) collective-permute-start(f32[1,1536]{1,0:T(1,128)S(1)} %shard_map.68.refs_1_.refs_2_), channel_id=1, source_target_pairs={{0,1},{1,0},{2,3},{3,2},{4,5},{5,4},{6,7},{7,6},{8,9},{9,8},{10,11... | collective-permute-start | bytes 18440 | tf_op jit(solution)/shard_map/ppermute | solution.py:171
  21.7 3.4 %collective-permute-start.11 = (s32[1,16]{1,0:T(1,128)S(1)}, s32[1,16]{1,0:T(1,128)S(1)}, u32[]{:S(2)}, u32[]{:S(2)}) collective-permute-start(s32[1,16]{1,0:T(1,128)S(1)} %collective-permute-done.7.refs_6_), channel_id=1, source_target_pairs={{0,3},{1,4},{2,7},{3,0},{4,1},{5,8},{6,11},{7,2},{8,5},{9,12},{10,... | collective-permute-start | bytes 200 | tf_op jit(solution)/shard_map/ppermute | solution.py:171
  25.1 5.2 %collective-permute-start.10 = (s32[1,16]{1,0:T(1,128)S(1)}, s32[1,16]{1,0:T(1,128)S(1)}, u32[]{:S(2)}, u32[]{:S(2)}) collective-permute-start(s32[1,16]{1,0:T(1,128)S(1)} %collective-permute-done.6.refs_5_), channel_id=1, source_target_pairs={{0,3},{1,4},{2,7},{3,0},{4,1},{5,8},{6,11},{7,2},{8,5},{9,12},{10,... | collective-permute-start | bytes 200 | tf_op jit(solution)/shard_map/ppermute | solution.py:171
  25.6 15.8 %collective-permute-start.15 = (s32[1,16]{1,0:T(1,128)S(1)}, s32[1,16]{1,0:T(1,128)S(1)}, u32[]{:S(2)}, u32[]{:S(2)}) collective-permute-start(s32[1,16]{1,0:T(1,128)S(1)} %collective-permute-done.11.refs_9_), channel_id=1, source_target_pairs={{0,5},{1,2},{2,1},{3,6},{4,9},{5,0},{6,3},{7,10},{8,13},{9,4},{10,... | collective-permute-start | bytes 200 | tf_op jit(solution)/shard_map/ppermute | solution.py:171
  27.3 14.1 %collective-permute-start.12 = (bf16[128,1024]{1,0:T(8,128)(2,1)S(1)}, bf16[128,1024]{1,0:T(8,128)(2,1)S(1)}, u32[]{:S(2)}, u32[]{:S(2)}) collective-permute-start(bf16[128,1024]{1,0:T(8,128)(2,1)S(1)} %collective-permute-done.8.refs_6_), channel_id=1, source_target_pairs={{0,5},{1,2},{2,1},{3,6},{4,9},{5,0},{6,3},{7,10},{8,13},{9,4},{10,... | collective-permute-start | bytes 786440 | tf_op jit(solution)/shard_map/ppermute | solution.py:171
  27.4 14.0 %collective-permute-start.13 = (bf16[128,1024]{1,0:T(8,128)(2,1)S(1)}, bf16[128,1024]{1,0:T(8,128)(2,1)S(1)}, u32[]{:S(2)}, u32[]{:S(2)}) collective-permute-start(bf16[128,1024]{1,0:T(8,128)(2,1)S(1)} %collective-permute-done.9.refs_7_), channel_id=1, source_target_pairs={{0,5},{1,2},{2,1},{3,6},{4,9},{5,0},{6,3},{7,10},{8,13},{9,4},{10,... | collective-permute-start | bytes 786440 | tf_op jit(solution)/shard_map/ppermute | solution.py:171
  30.3 5.6 %collective-permute-start.14 = (f32[2,128]{1,0:T(2,128)S(1)}, f32[2,128]{1,0:T(2,128)S(1)}, u32[]{:S(2)}, u32[]{:S(2)}) collective-permute-start(f32[2,128]{1,0:T(2,128)S(1)} %fusion), channel_id=1, source_target_pairs={{0,5},{1,2},{2,1},{3,6},{4,9},{5,0},{6,3},{7,10},{8,13},{9,4},{10,... | collective-permute-start | bytes 3080 | tf_op jit(solution)/shard_map/ppermute | solution.py:171
  36.0 4.4 %collective-permute-start.16 = (f32[2,128]{1,0:T(2,128)S(1)}, f32[2,128]{1,0:T(2,128)S(1)}, u32[]{:S(2)}, u32[]{:S(2)}) collective-permute-start(f32[2,128]{1,0:T(2,128)S(1)} %pad_maximum_fusion), channel_id=1, source_target_pairs={{0,3},{1,4},{2,7},{3,0},{4,1},{5,8},{6,11},{7,2},{8,5},{9,12},{10,... | collective-permute-start | bytes 3080 | tf_op jit(solution)/shard_map/ppermute | solution.py:171
  40.4 3.1 %collective-permute-start.17 = (f32[2,128]{1,0:T(2,128)S(1)}, f32[2,128]{1,0:T(2,128)S(1)}, u32[]{:S(2)}, u32[]{:S(2)}) collective-permute-start(f32[2,128]{1,0:T(2,128)S(1)} %pad_maximum_fusion.1), channel_id=1, source_target_pairs={{0,5},{1,2},{2,1},{3,6},{4,9},{5,0},{6,3},{7,10},{8,13},{9,4},{10,... | collective-permute-start | bytes 3080 | tf_op jit(solution)/shard_map/ppermute | solution.py:171
  41.4 11.5 %copy-start.3 = (f32[1536]{0:T(1024)S(1)}, f32[1536]{0:T(1024)}, u32[]{:S(2)}) copy-start(f32[1536]{0:T(1024)} %param.6) | copy-start | bytes 18436
  43.5 6.4 %collective-permute-start.19 = (f32[1,128]{1,0:T(1,128)S(1)}, f32[1,128]{1,0:T(1,128)S(1)}, u32[]{:S(2)}, u32[]{:S(2)}) collective-permute-start(f32[1,128]{1,0:T(1,128)S(1)} %get-tuple-element.35), channel_id=1, source_target_pairs={{0,13},{1,10},{2,9},{3,14},{4,15},{5,6},{6,5},{7,12},{8,11},{9,2},... | collective-permute-start | bytes 1544 | tf_op jit(solution)/shard_map/ppermute | solution.py:171
  46.1 6.3 %collective-permute-start.18 = (f32[1,128]{1,0:T(1,128)S(1)}, f32[1,128]{1,0:T(1,128)S(1)}, u32[]{:S(2)}, u32[]{:S(2)}) collective-permute-start(f32[1,128]{1,0:T(1,128)S(1)} %get-tuple-element.34), channel_id=1, source_target_pairs={{0,14},{1,15},{2,12},{3,13},{4,10},{5,11},{6,8},{7,9},{8,6},{9,7},... | collective-permute-start | bytes 1544 | tf_op jit(solution)/shard_map/ppermute | solution.py:171
  48.5 4.4 %collective-permute-start.20 = (f32[1536]{0:T(1024)S(1)}, f32[1536]{0:T(1024)S(1)}, u32[]{:S(2)}, u32[]{:S(2)}) collective-permute-start(f32[1536]{0:T(1024)S(1)} %reduce_max.19), channel_id=1, source_target_pairs={{0,1},{1,0},{2,3},{3,2},{4,5},{5,4},{6,7},{7,6},{8,9},{9,8},{10,11... | collective-permute-start | bytes 18440 | tf_op jit(solution)/shard_map/ppermute | solution.py:171
